TPU v7x, 256 devices: a whole 4x4x8 slice. The times are simulated.
256 devices in a mesh: cohort: 4 (over x), dev: 64 (over z, y, core).
Axes of the slice: x: 4, y: 4, z: 8, core: 2. Of those that a mesh axis runs over, the one named last changes fastest.
Arguments:
- dosage: bfloat16 [524288, 2048], P(('cohort', 'dev')), may hold values from 0 to 2
- allele_freq: float32 [2048], replicated, may hold values from 0.05 to 0.5
- probes: bfloat16 [2048, 512], replicated, may hold values from -6 to 6
- owner_perm: int32 [2048], replicated, may hold values from 0 to 2047, each once
Outputs:
- projected: float32 [2048, 512], P('dev')
Inputs may be any that keep to these rules, and one draw needn't show every extreme that they name: `owner_perm`: each SNP appears exactly once.
All inputs are finite; a program needn't handle non-finite values.
Results may differ from a plain program's by a relative error of at most 0.00044.
Values sent between devices are 32-bit elements; how exact they have to be, the bound alone decides.
No kernel may reach another device: no remote copies, remote signals or barrier semaphores. Data moves between devices by JAX's collectives and lax.ppermute only.
A program may use at most 128 MiB of HBM per device.

v0:
```python
import jax
import jax.numpy as jnp
from jax import lax
from jax.sharding import PartitionSpec as P


def body(dosage, allele_freq, probes, owner_perm):
    mean_dose = 2.0 * allele_freq
    inv_spread = 1.0 / jnp.sqrt(2.0 * allele_freq * (1.0 - allele_freq))
    centered = ((dosage.astype(jnp.float32) - mean_dose[None, :]) * inv_spread[None, :]).astype(
        jnp.bfloat16
    )
    sketch = jnp.dot(centered, probes, preferred_element_type=jnp.float32)
    local_gram = jnp.dot(sketch.T, sketch, precision=lax.Precision.HIGHEST)
    gram = lax.psum(local_gram, ("cohort", "dev"))
    lower = jnp.linalg.cholesky(gram)
    basis_t = lax.linalg.triangular_solve(lower, sketch.T, left_side=True, lower=True).astype(
        jnp.bfloat16
    )
    picked = jnp.take(centered, owner_perm, axis=1)
    owned = lax.psum_scatter(
        lax.dot_general(
            picked, basis_t, (((0,), (1,)), ((), ())), preferred_element_type=jnp.float32
        ),
        "dev",
        scatter_dimension=0,
        tiled=True,
    )
    return lax.psum(owned, "cohort")


def solution(mesh):
    return jax.shard_map(
        body,
        mesh=mesh,
        in_specs=(P(("cohort", "dev"), None), P(), P(), P()),
        out_specs=P("dev", None),
        check_vma=False,
    )
```

profile of v0, /device:TPU:8, one launch (start us, length us, event | category | flops | bytes accessed | tf_op | source)
XLA Modules:
  0.0 672.8 jit_solution(805267399925746850)
XLA Ops:
  7.4 12.3 %copy.5 = bf16[2048,2048]{0,1:T(8,128)(2,1)} copy(bf16[2048,2048]{1,0:T(8,128)(2,1)} %param.4) | data formatting | bytes 16777216 | tf_op args[0]
  19.7 5.2 multiply_convert_fusion
  24.9 4.6 fusion.51
  29.5 1.9 copy-done.2
  31.4 7.9 %fusion.52 = f32[512,512]{0,1:T(8,128)} fusion(f32[2048,512]{1,0:T(8,128)S(1)} %fusion.51), kind=kOutput, calls=%fused_computation.91 | convolution fusion | flops 6442450944 | bytes 5242880 | tf_op jit(solution)/shard_map/dot_general | solution.py:14
  39.7 20.8 %gather_fusion = bf16[2048,2048]{1,0:T(8,128)(2,1)} fusion(bf16[2048,2048]{0,1:T(8,128)(2,1)} %copy-done.1, s32[2048]{0:T(1024)S(1)} %fusion.42), kind=kCustom, calls=%fused_computation | custom fusion | bytes 16785408 | tf_op jit(solution)/shard_map/jit(_take)/gather | solution.py:20
  60.5 240.5 %all-reduce.4.cloned.1.call-done = f32[512,512]{0,1:T(8,128)} async-done(((f32[512,512]{0,1:T(8,128)}), f32[512,512]{0,1:T(8,128)}) %all-reduce.4.cloned.1.call-update) | async-done | bytes 1048592 | tf_op jit(solution)/shard_map/psum | solution.py:15
  301.1 1.6 copy.7
  302.6 1.4 fusion.25
  305.1 11.7 %cholesky.104 = f32[128,128]{1,0:T(8,128)S(1)} custom-call(f32[128,128]{1,0:T(8,128)S(1)} %cholesky.266), custom_call_target="Cholesky" | custom-call | tf_op jit(solution)/shard_map/jit(cholesky)/cholesky | solution.py:16
  316.9 9.8 %custom-call.30 = f32[1,128,128]{1,2,0:T(8,128)S(1)} custom-call(f32[1,128,128]{2,1,0:T(8,128)S(1)} %get-tuple-element.32), custom_call_target="InvertDiagBlocksLowerTriangular" | custom-call | tf_op jit(solution)/shard_map/jit(cholesky)/cholesky | solution.py:16
  329.4 11.7 %cholesky.217 = f32[128,128]{1,0:T(8,128)S(1)} custom-call(f32[128,128]{1,0:T(8,128)S(1)} %cholesky.270), custom_call_target="Cholesky" | custom-call | tf_op jit(solution)/shard_map/jit(cholesky)/cholesky | solution.py:16
  341.1 10.0 %custom-call.31 = f32[1,128,128]{1,2,0:T(8,128)S(1)} custom-call(f32[1,128,128]{2,1,0:T(8,128)S(1)} %get-tuple-element.29), custom_call_target="InvertDiagBlocksLowerTriangular" | custom-call | tf_op jit(solution)/shard_map/jit(cholesky)/cholesky | solution.py:16
  351.3 1.3 convolution_subtract_fusion.3
  352.6 11.7 %cholesky.238 = f32[128,128]{1,0:T(8,128)S(1)} custom-call(f32[128,128]{1,0:T(8,128)S(1)} %cholesky.275), custom_call_target="Cholesky" | custom-call | tf_op jit(solution)/shard_map/jit(cholesky)/cholesky | solution.py:16
  365.1 9.8 %custom-call.32 = f32[1,128,128]{1,2,0:T(8,128)S(1)} custom-call(f32[1,128,128]{2,1,0:T(8,128)S(1)} %get-tuple-element.26), custom_call_target="InvertDiagBlocksLowerTriangular" | custom-call | tf_op jit(solution)/shard_map/jit(cholesky)/cholesky | solution.py:16
  376.3 11.7 %cholesky.255 = f32[128,128]{1,0:T(8,128)S(1)} custom-call(f32[128,128]{1,0:T(8,128)S(1)} %convolution_subtract_fusion.4), custom_call_target="Cholesky" | custom-call | tf_op jit(solution)/shard_map/jit(cholesky)/cholesky | solution.py:16
  391.9 1.4 select_select_fusion
  393.3 13.8 %while.1 = (s32[]{:T(128)}, f32[512,512]{1,0:T(8,128)}, s32[4,2]{0,1:T(2,128)S(1)}, f32[4,128,128]{2,1,0:T(8,128)}, s32[]{:T(128)}) while((s32[]{:T(128)}, f32[512,512]{1,0:T(8,128)}, s32[4,2]{0,1:T(2,128)S(1)}, f32[4,128,128]{2,1,0:T(8,128)}, s32[]{:T(128)}) %tuple.31), condition=%wide.while_cond, body=%wide.while_body.sunk | while | flops 2 | bytes 132705 | solution.py:17
  393.9 2.8 bitcast_dynamic-update-slice_fusion.2
  397.4 2.8 bitcast_dynamic-update-slice_fusion.2
  400.9 2.8 bitcast_dynamic-update-slice_fusion.2
  404.3 2.8 bitcast_dynamic-update-slice_fusion.2
  407.1 40.1 %custom-call.33 = f32[4,128,128]{1,2,0:T(8,128)S(1)} custom-call(f32[4,128,128]{2,1,0:T(8,128)} %get-tuple-element.12), custom_call_target="InvertDiagBlocksLowerTriangular" | custom-call | tf_op jit(solution)/shard_map/triangular_solve | solution.py:17
  447.2 2.4 fusion.50
  449.7 3.1 convolution_subtract_fusion.1
  453.9 4.6 convolution_subtract_fusion
  459.6 6.7 fusion.10
  467.4 6.5 fusion
  474.0 142.6 %reduce-scatter.2.cloned.1.call-done = f32[32,512]{1,0:T(8,128)} async-done(((f32[2048,512]{1,0:T(8,128)}), f32[32,512]{1,0:T(8,128)}) %reduce-scatter.2.cloned.1.call-update) | async-done | bytes 65552 | tf_op jit(solution)/shard_map/reduce_scatter | solution.py:21
  616.6 47.7 %all-reduce.6.cloned.1.call-done = f32[32,512]{1,0:T(8,128)} async-done(((f32[32,512]{1,0:T(8,128)}), f32[32,512]{1,0:T(8,128)}) %all-reduce.6.cloned.1.call-update) | async-done | bytes 65552 | tf_op jit(solution)/shard_map/psum | solution.py:29
  664.3 1.5 copy.26
  (55 shorter events, 14.7 us)
Async XLA Ops:
  6.5 18.3 %copy-start = (bf16[2048,512]{1,0:T(8,128)(2,1)S(1)}, bf16[2048,512]{1,0:T(8,128)(2,1)}, u32[]{:S(2)}) copy-start(bf16[2048,512]{1,0:T(8,128)(2,1)} %param.6) | copy-start | bytes 6291460
  6.5 294.5 %all-reduce.4.cloned.1.call-start = ((), (), s32[]{:S(2)}) async-start(), calls=%async_computation.1 | async-start | bytes 2097152 | tf_op jit(solution)/shard_map/psum | solution.py:15
  24.9 4.6 copy-start.1
  29.5 1.9 copy-start.2
  31.4 8.3 %copy-start.5 = (s32[2048]{0:T(1024)S(1)}, s32[2048]{0:T(1024)}, u32[]{:S(2)}) copy-start(s32[2048]{0:T(1024)} %param.7) | copy-start | bytes 24580
  39.3 577.3 %reduce-scatter.2.cloned.1.call-start = ((), (), s32[]{:S(2)}) async-start(), calls=%async_computation.2 | async-start | bytes 4259840 | tf_op jit(solution)/shard_map/reduce_scatter | solution.py:21
  304.1 1.1 copy-start.4
  447.2 6.6 copy-start.3
  452.8 14.6 %slice-start = ((s8[8388608]{0:T(1024)(128)(4,1)}), s8[4194304]{0:T(1024)(128)(4,1)S(1)}, s32[]{:S(2)}) async-start(s8[8388608]{0:T(1024)(128)(4,1)} %bitcast.63), calls=%async_computation.4 | async-start | bytes 8388608
  458.5 8.9 %slice-start.1 = ((s8[8388608]{0:T(1024)(128)(4,1)}), s8[4194304]{0:T(1024)(128)(4,1)S(1)}, s32[]{:S(2)}) async-start(s8[8388608]{0:T(1024)(128)(4,1)} %bitcast.63), calls=%async_computation.5 | async-start | bytes 8388608
  473.9 190.4 %all-reduce.6.cloned.1.call-start = ((), (), s32[]{:S(2)}) async-start(), calls=%async_computation.3 | async-start | bytes 131072 | tf_op jit(solution)/shard_map/psum | solution.py:29
Sparse Core Ops, SparseCore 0:
  39.4 261.6 all-reduce.3
  474.0 142.4 reduce-scatter.1
  618.9 45.4 all-reduce.5
where the time goes:
time: 682 us; the launch traced here: 673 us
  waiting for transfers between devices  431 us (63%)
  other arithmetic  128 us (19%)
  local copies, waits for them, and re-layouts  53.1 us (8%)
  matrix products  44.4 us (7%)
  between operations  16.3 us (2%)
    psum x1, waiting for transfers between devices, body(): gram = lax.psum(local_gram, ('cohort', 'dev'))  241 us
    reduce_scatter x1, waiting for transfers between devices, body(): lax.psum_scatter(lax.dot_general(picked, basis_t, (((0,), (1,)), ((), ())...  143 us
    another operation x14, other arithmetic, body(): lower = jnp.linalg.cholesky(gram)  78.6 us
    psum x1, waiting for transfers between devices, body(): return lax.psum(owned, 'cohort')  47.7 us
    another operation x3, other arithmetic, body(): lax.linalg.triangular_solve(lower, sketch.T, left_side=True, lower=True)  41.5 us
    gather x1, local copies, waits for them, and re-layouts, body(): picked = jnp.take(centered, owner_perm, axis=1)  20.8 us
    another operation x7, matrix products, body(): lax.linalg.triangular_solve(lower, sketch.T, left_side=True, lower=True)  20 us
    unnamed x18, local copies, waits for them, and re-layouts  16.8 us
  transfers between devices with their start and end apart: 3, of which 3 were waited for; matrix products, arithmetic and copies ran while one was open for 3% of the time, Pallas kernels for 0%

commit v1 on v0

v1 whole, which is shorter than its diff:
```python
import functools

import jax
import jax.numpy as jnp
from jax import lax
from jax.experimental import pallas as pl
from jax.experimental.pallas import tpu as pltpu
from jax.sharding import Mesh, PartitionSpec as P


NX, NZ, NY, NC = 4, 8, 4, 2
B = 128
NB = 4
PAIRS = [(i, j) for i in range(NB) for j in range(i, NB)]
TN = (((0,), (0,)), ((), ()))


def dot(a, b, dims):
    return lax.dot_general(a, b, dims, preferred_element_type=jnp.float32)


def sketch_kernel(d_ref, m_ref, s_ref, p_ref, hi_ref, lo_ref, g_ref):
    c = ((d_ref[...].astype(jnp.float32) - m_ref[...]) * s_ref[...]).astype(jnp.bfloat16)
    sketch = jnp.dot(c, p_ref[...], preferred_element_type=jnp.float32)
    hi = sketch.astype(jnp.bfloat16)
    lo = (sketch - hi.astype(jnp.float32)).astype(jnp.bfloat16)
    hi_ref[...] = hi
    lo_ref[...] = lo
    first = pl.program_id(0) == 0
    for p in range(NB):
        a, b = slice(p * B, (p + 1) * B), slice(p * B, None)
        strip = dot(hi[:, a], hi[:, b], TN) + dot(hi[:, a], lo[:, b], TN) + dot(lo[:, a], hi[:, b], TN)
        for t in range(NB - p):
            n = PAIRS.index((p, p + t))
            at = slice(n * B, (n + 1) * B)
            piece = strip[:, t * B : (t + 1) * B]

            @pl.when(first)
            def _():
                g_ref[at, :] = piece

            @pl.when(jnp.logical_not(first))
            def _():
                g_ref[at, :] += piece


def sketch_gram(dosage, mean, scale, probes, step=1024):
    n, m = dosage.shape
    k = probes.shape[1]
    whole = lambda i: (0, 0)
    return pl.pallas_call(
        sketch_kernel,
        grid=(n // step,),
        in_specs=[
            pl.BlockSpec((step, m), lambda i: (i, 0)),
            pl.BlockSpec((1, m), whole),
            pl.BlockSpec((1, m), whole),
            pl.BlockSpec((m, k), whole),
        ],
        out_specs=(
            pl.BlockSpec((step, k), lambda i: (i, 0)),
            pl.BlockSpec((step, k), lambda i: (i, 0)),
            pl.BlockSpec((len(PAIRS) * B, B), whole),
        ),
        out_shape=(
            jax.ShapeDtypeStruct((n, k), jnp.bfloat16),
            jax.ShapeDtypeStruct((n, k), jnp.bfloat16),
            jax.ShapeDtypeStruct((len(PAIRS) * B, B), jnp.float32),
        ),
        name="sketch_gram",
    )(dosage, mean, scale, probes)


def product_kernel(d_ref, m_ref, s_ref, hi_ref, lo_ref, w_ref):
    c = ((d_ref[...].astype(jnp.float32) - m_ref[...]) * s_ref[...]).astype(jnp.bfloat16)
    w_ref[...] = dot(c, hi_ref[...], TN) + dot(c, lo_ref[...], TN)


def product(dosage, mean, scale, hi, lo, step=256):
    n, m = dosage.shape
    k = hi.shape[1]
    whole = lambda i: (0, 0)
    return pl.pallas_call(
        product_kernel,
        grid=(m // step,),
        in_specs=[
            pl.BlockSpec((n, step), lambda i: (0, i)),
            pl.BlockSpec((1, step), lambda i: (0, i)),
            pl.BlockSpec((1, step), lambda i: (0, i)),
            pl.BlockSpec((n, k), whole),
            pl.BlockSpec((n, k), whole),
        ],
        out_specs=pl.BlockSpec((step, k), lambda i: (i, 0)),
        out_shape=jax.ShapeDtypeStruct((m, k), jnp.float32),
        name="product",
    )(dosage, mean, scale, hi, lo)


def gather_kernel(i_ref, w_ref, o_ref):
    def eight(r, _):
        base = pl.multiple_of(r * 8, 8)
        o_ref[pl.ds(base, 8), :] = jnp.concatenate(
            [w_ref[pl.ds(i_ref[base + s], 1), :] for s in range(8)], axis=0)
        return 0

    lax.fori_loop(0, o_ref.shape[0] // 8, eight, 0, unroll=2)


def gather_rows(index, rows):
    return pl.pallas_call(
        gather_kernel,
        out_shape=jax.ShapeDtypeStruct((index.shape[0], rows.shape[1]), rows.dtype),
        in_specs=[pl.BlockSpec(memory_space=pltpu.SMEM), pl.BlockSpec(memory_space=pltpu.VMEM)],
        out_specs=pl.BlockSpec(memory_space=pltpu.VMEM),
        name="gather_rows",
    )(index, rows)


HI = lax.Precision.HIGHEST
NT = (((1,), (1,)), ((), ()))


def factor_kernel(p, g_ref, *refs):
    prior = refs[:p]
    r_ref, inv_ref, s_ref = refs[p:]
    w = (NB - p) * B
    wide = w + B
    for t in range(NB - p):
        n = PAIRS.index((p, p + t))
        s_ref[:, t * B : (t + 1) * B] = g_ref[n * B : (n + 1) * B, :]
    for q in range(p):
        off = (p - q) * B
        s_ref[:, :w] -= lax.dot_general(
            prior[q][:, off : off + B], prior[q][:, off:], TN,
            precision=HI, preferred_element_type=jnp.float32)
    s_ref[:, w:] = (
        lax.broadcasted_iota(jnp.int32, (B, B), 0) == lax.broadcasted_iota(jnp.int32, (B, B), 1)
    ).astype(jnp.float32)
    for b in range(B // 8):
        lo = 8 * b
        rows = s_ref[lo : lo + 8, :]
        cols = [jnp.broadcast_to(rows[:, lo + m : lo + m + 1], (8, B)) for m in range(8)]
        e = [[jnp.broadcast_to(cols[m][j : j + 1, :], (8, B)) if j >= m else None
              for m in range(8)] for j in range(8)]
        u = [[jnp.broadcast_to(rows[j : j + 1, t * B : (t + 1) * B], (8, B))
              for t in range(wide // B)] for j in range(8)]
        inv = [None] * 8
        l = [[None] * 8 for _ in range(8)]
        for j in range(8):
            inv[j] = 1.0 / e[j][j]
            for m in range(j + 1, 8):
                l[m][j] = e[m][j] * inv[j]
            for m in range(j + 1, 8):
                for n in range(m, 8):
                    e[n][m] = e[n][m] - l[n][j] * e[m][j]
                u[m] = [a - l[m][j] * c for a, c in zip(u[m], u[j])]
        v = [[a * inv[j] for a in u[j]] for j in range(8)]
        for j in range(8):
            root = lax.rsqrt(e[j][j])
            root = root * (1.5 - 0.5 * e[j][j] * root * root)
            for t in range(wide // B):
                row = (u[j][t] * root)[0:1, :]
                if t < NB - p:
                    r_ref[lo + j : lo + j + 1, t * B : (t + 1) * B] = row
                else:
                    inv_ref[lo + j : lo + j + 1, :] = row
        for d in range(b + 1, B // 8):
            at = slice(8 * d, 8 * d + 8)
            tail = s_ref[at, :]
            cols = [jnp.broadcast_to(tail[:, lo + m : lo + m + 1], (8, B)) for m in range(8)]
            for j in range(8):
                for m in range(j + 1, 8):
                    cols[m] = cols[m] - cols[j] * l[m][j]
            for t in range(wide // B):
                x = tail[:, t * B : (t + 1) * B]
                y = cols[0] * v[0][t]
                z = cols[1] * v[1][t]
                for m in range(2, 8, 2):
                    y = y + cols[m] * v[m][t]
                    z = z + cols[m + 1] * v[m + 1][t]
                s_ref[at, t * B : (t + 1) * B] = x - (y + z)


def factor(p, packed, prior):
    w = (NB - p) * B
    vm = pl.BlockSpec(memory_space=pltpu.VMEM)
    return pl.pallas_call(
        functools.partial(factor_kernel, p),
        out_shape=(
            jax.ShapeDtypeStruct((B, w), jnp.float32),
            jax.ShapeDtypeStruct((B, B), jnp.float32),
        ),
        in_specs=[vm] * (1 + p),
        out_specs=(vm, vm),
        scratch_shapes=[pltpu.VMEM((B, w + B), jnp.float32)],
        cost_estimate=pl.CostEstimate(flops=10_000_000_000, bytes_accessed=1 << 20, transcendentals=0),
    )(packed, *prior)


def finish_kernel(w_ref, *refs):
    r, inv, x_ref = refs[:NB], refs[NB : 2 * NB], refs[2 * NB]
    for p in range(NB):
        acc = w_ref[:, p * B : (p + 1) * B]
        for q in range(p):
            acc = acc - lax.dot_general(
                x_ref[:, q * B : (q + 1) * B], r[q][:, (p - q) * B : (p - q + 1) * B],
                (((1,), (0,)), ((), ())), precision=HI, preferred_element_type=jnp.float32)
        x_ref[:, p * B : (p + 1) * B] = lax.dot_general(
            acc, inv[p][...], NT, precision=HI, preferred_element_type=jnp.float32)


def finish(owned, panels, inverses):
    vm = pl.BlockSpec(memory_space=pltpu.VMEM)
    return pl.pallas_call(
        finish_kernel,
        out_shape=jax.ShapeDtypeStruct(owned.shape, jnp.float32),
        in_specs=[vm] * (1 + 2 * NB),
        out_specs=vm,
        name="finish",
    )(owned, *panels, *inverses)


def shifted(value, axis, size, step):
    return lax.ppermute(value, axis, [(k, (k + step) % size) for k in range(size)])


def exchange(value, axis, size):
    total = value
    for s in range(1, size):
        total = total + shifted(value, axis, size, s)
    return total


def after(value, *others):
    return lax.optimization_barrier((value,) + others)


def row_order(owner_perm):
    _, _, y, c = (lax.axis_index(a) for a in ("x", "z", "y", "c"))
    ci, yi, zi, r = jnp.ix_(jnp.arange(NC), jnp.arange(NY), jnp.arange(NZ), jnp.arange(32))
    row = 32 * (zi * (NY * NC) + ((y + yi) % NY) * NC + (c + ci) % NC) + r
    return owner_perm.at[row.reshape(-1)].get(mode="promise_in_bounds")


def steps(dosage, allele_freq, probes, owner_perm):
    c = lax.axis_index("c")
    mean_dose = (2.0 * allele_freq)[None, :]
    inv_spread = (1.0 / jnp.sqrt(2.0 * allele_freq * (1.0 - allele_freq)))[None, :]
    order = row_order(owner_perm)
    high, low, packed = sketch_gram(dosage, mean_dose, inv_spread, probes)
    packed, order = after(packed, order)
    halves = packed.reshape(NC, -1, B)
    mine = lax.dynamic_index_in_dim(halves, c, 0, False)
    other = lax.dynamic_index_in_dim(halves, 1 - c, 0, False)
    half = mine + shifted(other, "c", NC, 1)
    half, high = after(half, high)
    part = half.reshape(NX * NZ, -1, B)
    part = lax.all_to_all(part, ("x", "z"), 0, 0, tiled=True)
    rows = product(dosage, mean_dose, inv_spread, high, low)
    part = part.sum(0)
    part, rows = after(part, rows)
    total = exchange(part, "y", NY)
    away = gather_rows(order[1024:], rows)
    total, away, rows = after(total, away, rows)
    came = shifted(away, "c", NC, 1)
    spread = jnp.broadcast_to(total[None], (NX * NZ,) + total.shape)
    half = lax.all_to_all(spread, ("x", "z"), 0, 0, tiled=True).reshape(-1, B)
    kept = gather_rows(order[:1024], rows)
    half, kept, came = after(half, kept, came)
    other = shifted(half, "c", NC, 1)
    packed = jnp.concatenate(
        [jnp.where(c == 0, half, other), jnp.where(c == 0, other, half)], axis=0
    )
    k = rows.shape[1]
    packed, block = after(packed, (kept + came).reshape(NY, -1, k))
    sent = []
    for s in range(1, NY):
        sent.append(shifted(block[s], "y", NY, s))
    panels, inverses = [], []
    for p in range(NB):
        r, inv = factor(p, packed, panels)
        panels.append(r)
        inverses.append(inv)
    owned = block[0]
    for part in sent:
        owned = owned + part
    owned = lax.all_to_all(owned.reshape(NZ, -1, k), "z", 0, 0, tiled=True)
    owned = exchange(owned.sum(0), "x", NX)
    return finish(owned, panels, inverses)


def solution(mesh):
    torus = Mesh(mesh.devices.reshape(NX, NZ, NY, NC), ("x", "z", "y", "c"))
    return jax.shard_map(
        steps,
        mesh=torus,
        in_specs=(P(("x", "z", "y", "c"), None), P(), P(), P()),
        out_specs=P(("z", "y", "c"), None),
        check_vma=False,
    )
```

time: 682 us -> 172 us (0.25); the launches traced: 673 us -> 171 us
  waiting for transfers between devices: 431 us -> 35.4 us
  other arithmetic: 128 us -> 9.07 us
  Pallas kernels: 0 us -> 71.1 us
  matrix products: 44.4 us -> 0 us
  starting transfers between devices: 0.43 us -> 37.5 us
  local copies, waits for them, and re-layouts: 53.1 us -> 17.4 us
  between operations: 16.3 us -> 0.18 us
    psum x2 -> x0, waiting for transfers between devices: 288 us -> none  [the longest x1 241 us: body(): gram = lax.psum(local_gram, ('cohort', 'dev'))]
    reduce_scatter x1 -> x0, waiting for transfers between devices: 143 us -> none  [body(): lax.psum_scatter(lax.dot_general(picked, basis_t, (((0,), (1,)), ((), ())...]
    another operation x17 -> x0, other arithmetic: 120 us -> none  [the longest x14 78.6 us: body(): lower = jnp.linalg.cholesky(gram)]
    pallas_call x0 -> x9, Pallas kernels: none -> 71.1 us  [the longest x4 27.4 us: factor(): pl.pallas_call(functools.partial(factor_kernel, p), out_shape=(jax.ShapeD...]
    another operation x13 -> x0, matrix products: 25.5 us -> none  [the longest x7 20 us: body(): lax.linalg.triangular_solve(lower, sketch.T, left_side=True, lower=True)]
    all_to_all x0 -> x3, starting transfers between devices: none -> 25.3 us  [the longest x1 11.3 us: steps(): part = lax.all_to_all(part, ('x', 'z'), 0, 0, tiled=True)]
    dot_general x3 -> x0, matrix products: 18.9 us -> none  [the longest x1 7.86 us: body(): local_gram = jnp.dot(sketch.T, sketch, precision=lax.Precision.HIGHEST)]
    all_to_all x0 -> x3, waiting for transfers between devices: none -> 18.2 us  [the longest x1 9.28 us: steps(): owned = lax.all_to_all(owned.reshape(NZ, -1, k), 'z', 0, 0, tiled=True)]
  transfers between devices with their start and end apart: 3 -> 15, of which waited for: 3 -> 6; matrix products, arithmetic and copies ran while one was open for 3% -> 2% of each run, Pallas kernels for 0% -> 27%
where the time goes in v1:
time: 172 us; the launch traced here: 171 us
  Pallas kernels  71.1 us (41%)
  starting transfers between devices  37.5 us (22%)
  waiting for transfers between devices  35.4 us (21%)
  local copies, waits for them, and re-layouts  17.4 us (10%)
  other arithmetic  9.07 us (5%)
    pallas_call x4, Pallas kernels, factor(): pl.pallas_call(functools.partial(factor_kernel, p), out_shape=(jax.ShapeD...  27.4 us
    ppermute x12, waiting for transfers between devices, shifted(): lax.ppermute(value, axis, [(k, (k + step) % size) for k in range(size)])  17.1 us
    pallas_call x1, Pallas kernels, product(): pl.pallas_call(product_kernel, grid=(m // step,), in_specs=[pl.BlockSpec(...  14.2 us
    pallas_call x1, Pallas kernels, sketch_gram(): pl.pallas_call(sketch_kernel, grid=(n // step,), in_specs=[pl.BlockSpec((...  14.1 us
    ppermute x12, starting transfers between devices, shifted(): lax.ppermute(value, axis, [(k, (k + step) % size) for k in range(size)])  12.2 us
    pallas_call x2, Pallas kernels, gather_rows(): pl.pallas_call(gather_kernel, out_shape=jax.ShapeDtypeStruct((index.shape...  11.9 us
    gather x1, local copies, waits for them, and re-layouts, row_order(): return owner_perm.at[row.reshape(-1)].get(mode='promise_in_bounds')  11.8 us
    all_to_all x1, starting transfers between devices, steps(): part = lax.all_to_all(part, ('x', 'z'), 0, 0, tiled=True)  11.3 us
  transfers between devices with their start and end apart: 15, of which 6 were waited for; matrix products, arithmetic and copies ran while one was open for 2% of the time, Pallas kernels for 27%

profile of v1, /device:TPU:8, one launch (start us, length us, event | category | flops | bytes accessed | tf_op | source)
XLA Modules:
  0.0 170.6 jit_solution(11388953315753141711)
XLA Ops:
  0.0 1.3 multiply_rsqrt_fusion
  1.7 11.8 %gather_fusion = s32[2048]{0:T(1024)S(1)} fusion(s32[2048]{0:T(1024)S(1)} %copy-done, s32[2048]{0:T(1024)S(1)} %broadcast_clamp_fusion), kind=kCustom, calls=%fused_computation | custom fusion | bytes 24576 | tf_op jit(solution)/shard_map/gather | solution.py:242
  13.5 14.1 %sketch_gram.1 = (bf16[2048,512]{1,0:T(8,128)(2,1)}, bf16[2048,512]{1,0:T(8,128)(2,1)}, f32[1280,128]{1,0:T(8,128)}) custom-call(bf16[2048,2048]{1,0:T(8,128)(2,1)} %d_ref.3, f32[1,2048]{1,0:T(1,128)} %bitcast.30, f32[1,2048]{1,0:T(1,128)} %bitcast.28, bf16[2048,512]{1,0:T(8,128)(2,1)} %p_ref.1), custom_call_target="tpu_custom_call" | custom-call | tf_op jit(solution)/shard_map/sketch_gram/pallas_call | solution.py:51
  27.6 1.0 dynamic-slice_bitcast_fusion
  28.7 1.6 collective-permute-done
  30.3 1.0 bitcast_add_fusion.1
  32.1 11.3 %all-to-all-start = ((f32[32,20,128]{2,1,0:T(8,128)}), f32[32,20,128]{2,1,0:T(8,128)S(1)}, u32[]{:S(2)}, u32[]{:S(2)}) async-start(f32[32,20,128]{2,1,0:T(8,128)} %reshape.142), calls=%async_computation | async-start | bytes 786432 | tf_op jit(solution)/shard_map/all_to_all | solution.py:258
  43.5 14.2 %product.1.w_ref = f32[2048,512]{1,0:T(8,128)} custom-call(bf16[2048,2048]{1,0:T(8,128)(2,1)} %d_ref.3, f32[1,2048]{1,0:T(1,128)} %bitcast.31, f32[1,2048]{1,0:T(1,128)} %bitcast.29, bf16[2048,512]{1,0:T(8,128)(2,1)} %get-tuple-element.34.hi_ref, bf16[2048,512]{1,0:T(8,128)(2,1)} %get-tuple-element.35.lo_ref), custom_call_target="tpu_custom_call" | custom-call | tf_op jit(solution)/shard_map/product/pallas_call | solution.py:83
  58.4 2.6 %collective-permute-start.2 = (f32[20,128]{1,0:T(8,128)S(1)}, f32[20,128]{1,0:T(8,128)S(1)}, u32[]{:S(2)}, u32[]{:S(2)}) collective-permute-start(f32[20,128]{1,0:T(8,128)S(1)} %reduce_sum.18), channel_id=1, source_target_pairs={{0,4},{2,6},{4,0},{6,2},{1,5},{3,7},{5,1},{7,3},{8,12},{10,14},{12... | collective-permute-start | bytes 30728 | tf_op jit(solution)/shard_map/ppermute | solution.py:224
  61.0 1.9 %collective-permute-start.1 = (f32[20,128]{1,0:T(8,128)S(1)}, f32[20,128]{1,0:T(8,128)S(1)}, u32[]{:S(2)}, u32[]{:S(2)}) collective-permute-start(f32[20,128]{1,0:T(8,128)S(1)} %reduce_sum.18), channel_id=1, source_target_pairs={{0,2},{2,4},{4,6},{6,0},{1,3},{3,5},{5,7},{7,1},{8,10},{10,12},{12... | collective-permute-start | bytes 30728 | tf_op jit(solution)/shard_map/ppermute | solution.py:224
  63.5 5.9 %gather_rows.2 = f32[1024,512]{1,0:T(8,128)} custom-call(s32[1024]{0:T(1024)} %get-tuple-element.61.i_ref, f32[2048,512]{1,0:T(8,128)} %product.1.w_ref), custom_call_target="tpu_custom_call" | custom-call | tf_op jit(solution)/shard_map/gather_rows/pallas_call | solution.py:110
  70.4 9.6 %all-to-all-start.1 = ((f32[32,20,128]{2,1,0:T(8,128)}), f32[32,20,128]{2,1,0:T(8,128)S(1)}, u32[]{:S(2)}, u32[]{:S(2)}) async-start(f32[32,20,128]{2,1,0:T(8,128)} %broadcast_in_dim.8), calls=%async_computation.1 | async-start | bytes 786432 | tf_op jit(solution)/shard_map/all_to_all | solution.py:267
  80.0 6.0 %gather_rows.3 = f32[1024,512]{1,0:T(8,128)} custom-call(s32[1024]{0:T(1024)} %get-tuple-element.60.i_ref, f32[2048,512]{1,0:T(8,128)} %product.1.w_ref), custom_call_target="tpu_custom_call" | custom-call | tf_op jit(solution)/shard_map/gather_rows/pallas_call | solution.py:110
  86.0 8.8 %all-to-all-done.1 = f32[32,20,128]{2,1,0:T(8,128)S(1)} async-done(((f32[32,20,128]{2,1,0:T(8,128)}), f32[32,20,128]{2,1,0:T(8,128)S(1)}, u32[]{:S(2)}, u32[]{:S(2)}) %all-to-all-start.1) | async-done | bytes 327712 | tf_op jit(solution)/shard_map/all_to_all | solution.py:267
  95.1 1.0 copy-done.1
  96.1 2.7 %add.182 = f32[1024,512]{1,0:T(8,128)S(1)} add(f32[1024,512]{1,0:T(8,128)} %gather_rows.3, f32[1024,512]{1,0:T(8,128)} %copy-done.1) | non-fusion elementwise | flops 524288 | bytes 6291456 | tf_op jit(solution)/shard_map/add | solution.py:275
  98.9 0.9 pad_maximum_fusion.g_ref
  99.8 6.8 %shard_map.46 = (f32[128,512]{1,0:T(8,128)}, f32[128,128]{1,0:T(8,128)}) custom-call(f32[1280,128]{1,0:T(8,128)} %pad_maximum_fusion.g_ref), custom_call_target="tpu_custom_call" | custom-call | flops 10000000000 | bytes 1048576 | tf_op jit(solution)/shard_map/pallas_call | solution.py:187
  106.6 1.2 slice_bitcast_fusion.2
  107.9 2.0 %collective-permute-start.8 = (f32[256,512]{1,0:T(8,128)}, f32[256,512]{1,0:T(8,128)S(1)}, u32[]{:S(2)}, u32[]{:S(2)}) collective-permute-start(f32[256,512]{1,0:T(8,128)} %get-tuple-element.56), channel_id=1, source_target_pairs={{0,6},{2,0},{4,2},{6,4},{1,7},{3,1},{5,3},{7,5},{8,14},{10,8},{12,... | collective-permute-start | bytes 1572872 | tf_op jit(solution)/shard_map/ppermute | solution.py:224
  109.9 1.2 collective-permute-start.7
  111.2 7.0 %shard_map.47 = (f32[128,384]{1,0:T(8,128)}, f32[128,128]{1,0:T(8,128)}) custom-call(f32[1280,128]{1,0:T(8,128)} %pad_maximum_fusion.g_ref, f32[128,512]{1,0:T(8,128)} %get-tuple-element.47.refs_0_), custom_call_target="tpu_custom_call" | custom-call | flops 10000000000 | bytes 1048576 | tf_op jit(solution)/shard_map/pallas_call | solution.py:187
  118.2 4.7 %collective-permute-done.6 = f32[256,512]{1,0:T(8,128)S(1)} collective-permute-done((f32[256,512]{1,0:T(8,128)}, f32[256,512]{1,0:T(8,128)S(1)}, u32[]{:S(2)}, u32[]{:S(2)}) %collective-permute-start.6) | collective-permute-done | bytes 524320 | tf_op jit(solution)/shard_map/ppermute | solution.py:224
  122.9 10.8 %collective-permute-done.7 = f32[256,512]{1,0:T(8,128)} collective-permute-done((f32[256,512]{1,0:T(8,128)}, f32[256,512]{1,0:T(8,128)}, u32[]{:S(2)}, u32[]{:S(2)}) %collective-permute-start.7) | collective-permute-done | bytes 524320 | tf_op jit(solution)/shard_map/ppermute | solution.py:224
  133.7 2.1 %fusion.1 = f32[256,512]{1,0:T(8,128)} fusion(f32[256,512]{1,0:T(8,128)S(1)} %collective-permute-done.8, f32[256,512]{1,0:T(8,128)} %collective-permute-done.7, f32[256,512]{1,0:T(8,128)S(1)} %collective-permute-done.6, f32[4,256,512]{2,1,0:T(8,128)S(1)} %bitcast.25), kind=kLoop, calls=%fused_computation.4 | loop fusion | flops 393216 | bytes 2621440 | tf_op jit(solution)/shard_map/add | solution.py:286
  135.8 4.4 %all-to-all-start.2 = ((f32[8,32,512]{2,1,0:T(8,128)}), f32[8,32,512]{2,1,0:T(8,128)S(1)}, u32[]{:S(2)}, u32[]{:S(2)}) async-start(f32[8,32,512]{2,1,0:T(8,128)} %bitcast.11), calls=%async_computation.2 | async-start | bytes 1048576 | tf_op jit(solution)/shard_map/all_to_all | solution.py:287
  140.2 6.9 %shard_map.48 = (f32[128,256]{1,0:T(8,128)}, f32[128,128]{1,0:T(8,128)}) custom-call(f32[1280,128]{1,0:T(8,128)} %pad_maximum_fusion.g_ref, f32[128,512]{1,0:T(8,128)} %get-tuple-element.47.refs_0_, f32[128,384]{1,0:T(8,128)} %get-tuple-element.48.refs_1_), custom_call_target="tpu_custom_call" | custom-call | flops 10000000000 | bytes 1048576 | tf_op jit(solution)/shard_map/pallas_call | solution.py:187
  147.0 9.3 %all-to-all-done.2 = f32[8,32,512]{2,1,0:T(8,128)S(1)} async-done(((f32[8,32,512]{2,1,0:T(8,128)}), f32[8,32,512]{2,1,0:T(8,128)S(1)}, u32[]{:S(2)}, u32[]{:S(2)}) %all-to-all-start.2) | async-done | bytes 524320 | tf_op jit(solution)/shard_map/all_to_all | solution.py:287
  156.3 1.5 collective-permute-start.11
  157.9 1.2 collective-permute-start.10
  159.8 6.6 %shard_map.49 = (f32[128,128]{1,0:T(8,128)}, f32[128,128]{1,0:T(8,128)}) custom-call(f32[1280,128]{1,0:T(8,128)} %pad_maximum_fusion.g_ref, f32[128,512]{1,0:T(8,128)} %get-tuple-element.47.refs_0_, f32[128,384]{1,0:T(8,128)} %get-tuple-element.48.refs_1_, f32[128,256]{1,0:T(8,128)} %get-tuple-element.49.refs_2_), custom_call_target="tpu_custom_call" | custom-call | flops 10000000000 | bytes 1048576 | tf_op jit(solution)/shard_map/pallas_call | solution.py:187
  167.1 3.5 %finish.1 = f32[32,512]{1,0:T(8,128)} custom-call(f32[32,512]{1,0:T(8,128)} %add_add_fusion.w_ref, f32[128,512]{1,0:T(8,128)} %get-tuple-element.47.refs_0_, f32[128,384]{1,0:T(8,128)} %get-tuple-element.48.refs_1_, f32[128,256]{1,0:T(8,128)} %get-tuple-element.49.refs_2_, f32[128,128]{1,0:T(8,128)} %get-tuple-element.50.refs_3_, ...), custom_call_target="tpu_custom_call" | custom-call | tf_op jit(solution)/shard_map/finish/pallas_call | solution.py:214
  (37 shorter events, 5.3 us)
Async XLA Ops:
  0.0 1.7 copy-start
  28.6 1.7 %collective-permute-start = (f32[640,128]{1,0:T(8,128)S(1)}, f32[640,128]{1,0:T(8,128)S(1)}, u32[]{:S(2)}, u32[]{:S(2)}) collective-permute-start(f32[640,128]{1,0:T(8,128)S(1)} %dynamic-slice_bitcast_fusion), channel_id=1, source_target_pairs={{0,1},{1,0},{2,3},{3,2},{4,5},{5,4},{6,7},{7,6},{8,9},{9,8},{10,11... | collective-permute-start | bytes 983048 | tf_op jit(solution)/shard_map/ppermute | solution.py:224
  32.1 25.7 %all-to-all-start = ((f32[32,20,128]{2,1,0:T(8,128)}), f32[32,20,128]{2,1,0:T(8,128)S(1)}, u32[]{:S(2)}, u32[]{:S(2)}) async-start(f32[32,20,128]{2,1,0:T(8,128)} %reshape.142), calls=%async_computation | async-start | bytes 786432 | tf_op jit(solution)/shard_map/all_to_all | solution.py:258
  57.9 11.5 %collective-permute-start.3 = (f32[20,128]{1,0:T(8,128)S(1)}, f32[20,128]{1,0:T(8,128)S(1)}, u32[]{:S(2)}, u32[]{:S(2)}) collective-permute-start(f32[20,128]{1,0:T(8,128)S(1)} %reduce_sum.18), channel_id=1, source_target_pairs={{0,6},{2,0},{4,2},{6,4},{1,7},{3,1},{5,3},{7,5},{8,14},{10,8},{12,... | collective-permute-start | bytes 30728 | tf_op jit(solution)/shard_map/ppermute | solution.py:224
  58.4 11.0 %collective-permute-start.2 = (f32[20,128]{1,0:T(8,128)S(1)}, f32[20,128]{1,0:T(8,128)S(1)}, u32[]{:S(2)}, u32[]{:S(2)}) collective-permute-start(f32[20,128]{1,0:T(8,128)S(1)} %reduce_sum.18), channel_id=1, source_target_pairs={{0,4},{2,6},{4,0},{6,2},{1,5},{3,7},{5,1},{7,3},{8,12},{10,14},{12... | collective-permute-start | bytes 30728 | tf_op jit(solution)/shard_map/ppermute | solution.py:224
  61.0 8.4 %collective-permute-start.1 = (f32[20,128]{1,0:T(8,128)S(1)}, f32[20,128]{1,0:T(8,128)S(1)}, u32[]{:S(2)}, u32[]{:S(2)}) collective-permute-start(f32[20,128]{1,0:T(8,128)S(1)} %reduce_sum.18), channel_id=1, source_target_pairs={{0,2},{2,4},{4,6},{6,0},{1,3},{3,5},{5,7},{7,1},{8,10},{10,12},{12... | collective-permute-start | bytes 30728 | tf_op jit(solution)/shard_map/ppermute | solution.py:224
  69.5 25.3 %collective-permute-start.4 = (f32[1024,512]{1,0:T(8,128)}, f32[1024,512]{1,0:T(8,128)S(1)}, u32[]{:S(2)}, u32[]{:S(2)}) collective-permute-start(f32[1024,512]{1,0:T(8,128)} %gather_rows.2), channel_id=1, source_target_pairs={{0,1},{1,0},{2,3},{3,2},{4,5},{5,4},{6,7},{7,6},{8,9},{9,8},{10,11... | collective-permute-start | bytes 6291464 | tf_op jit(solution)/shard_map/ppermute | solution.py:224
  70.4 24.4 %all-to-all-start.1 = ((f32[32,20,128]{2,1,0:T(8,128)}), f32[32,20,128]{2,1,0:T(8,128)S(1)}, u32[]{:S(2)}, u32[]{:S(2)}) async-start(f32[32,20,128]{2,1,0:T(8,128)} %broadcast_in_dim.8), calls=%async_computation.1 | async-start | bytes 786432 | tf_op jit(solution)/shard_map/all_to_all | solution.py:267
  94.8 1.3 copy-start.1
  94.8 4.0 %collective-permute-start.5 = (f32[640,128]{1,0:T(8,128)S(1)}, f32[640,128]{1,0:T(8,128)S(1)}, u32[]{:S(2)}, u32[]{:S(2)}) collective-permute-start(f32[640,128]{1,0:T(8,128)S(1)} %reshape.143), channel_id=1, source_target_pairs={{0,1},{1,0},{2,3},{3,2},{4,5},{5,4},{6,7},{7,6},{8,9},{9,8},{10,11... | collective-permute-start | bytes 983048 | tf_op jit(solution)/shard_map/ppermute | solution.py:224
  107.9 15.0 %collective-permute-start.6 = (f32[256,512]{1,0:T(8,128)}, f32[256,512]{1,0:T(8,128)S(1)}, u32[]{:S(2)}, u32[]{:S(2)}) collective-permute-start(f32[256,512]{1,0:T(8,128)} %get-tuple-element.55), channel_id=1, source_target_pairs={{0,2},{2,4},{4,6},{6,0},{1,3},{3,5},{5,7},{7,1},{8,10},{10,12},{12... | collective-permute-start | bytes 1572872 | tf_op jit(solution)/shard_map/ppermute | solution.py:224
  107.9 15.0 %collective-permute-start.8 = (f32[256,512]{1,0:T(8,128)}, f32[256,512]{1,0:T(8,128)S(1)}, u32[]{:S(2)}, u32[]{:S(2)}) collective-permute-start(f32[256,512]{1,0:T(8,128)} %get-tuple-element.56), channel_id=1, source_target_pairs={{0,6},{2,0},{4,2},{6,4},{1,7},{3,1},{5,3},{7,5},{8,14},{10,8},{12,... | collective-permute-start | bytes 1572872 | tf_op jit(solution)/shard_map/ppermute | solution.py:224
  109.9 23.8 %collective-permute-start.7 = (f32[256,512]{1,0:T(8,128)}, f32[256,512]{1,0:T(8,128)}, u32[]{:S(2)}, u32[]{:S(2)}) collective-permute-start(f32[256,512]{1,0:T(8,128)} %get-tuple-element.57), channel_id=1, source_target_pairs={{0,4},{2,6},{4,0},{6,2},{1,5},{3,7},{5,1},{7,3},{8,12},{10,14},{12... | collective-permute-start | bytes 1572872 | tf_op jit(solution)/shard_map/ppermute | solution.py:224
  135.8 20.5 %all-to-all-start.2 = ((f32[8,32,512]{2,1,0:T(8,128)}), f32[8,32,512]{2,1,0:T(8,128)S(1)}, u32[]{:S(2)}, u32[]{:S(2)}) async-start(f32[8,32,512]{2,1,0:T(8,128)} %bitcast.11), calls=%async_computation.2 | async-start | bytes 1048576 | tf_op jit(solution)/shard_map/all_to_all | solution.py:287
  156.3 10.1 %collective-permute-start.11 = (f32[32,512]{1,0:T(8,128)S(1)}, f32[32,512]{1,0:T(8,128)S(1)}, u32[]{:S(2)}, u32[]{:S(2)}) collective-permute-start(f32[32,512]{1,0:T(8,128)S(1)} %reduce_sum.19), channel_id=1, source_target_pairs={{0,192},{64,0},{128,64},{192,128},{1,193},{65,1},{129,65},{193,129... | collective-permute-start | bytes 196616 | tf_op jit(solution)/shard_map/ppermute | solution.py:224
  157.9 8.6 %collective-permute-start.10 = (f32[32,512]{1,0:T(8,128)S(1)}, f32[32,512]{1,0:T(8,128)S(1)}, u32[]{:S(2)}, u32[]{:S(2)}) collective-permute-start(f32[32,512]{1,0:T(8,128)S(1)} %reduce_sum.19), channel_id=1, source_target_pairs={{0,128},{64,192},{128,0},{192,64},{1,129},{65,193},{129,1},{193,65... | collective-permute-start | bytes 196616 | tf_op jit(solution)/shard_map/ppermute | solution.py:224
  159.1 7.4 %collective-permute-start.9 = (f32[32,512]{1,0:T(8,128)S(1)}, f32[32,512]{1,0:T(8,128)S(1)}, u32[]{:S(2)}, u32[]{:S(2)}) collective-permute-start(f32[32,512]{1,0:T(8,128)S(1)} %reduce_sum.19), channel_id=1, source_target_pairs={{0,64},{64,128},{128,192},{192,0},{1,65},{65,129},{129,193},{193,1... | collective-permute-start | bytes 196616 | tf_op jit(solution)/shard_map/ppermute | solution.py:224

commit v2 on v1

v2 whole, which is shorter than its diff:
```python
import functools

import jax
import jax.numpy as jnp
from jax import lax
from jax.experimental import pallas as pl
from jax.experimental.pallas import tpu as pltpu
from jax.sharding import Mesh, PartitionSpec as P


NX, NZ, NY, NC = 4, 8, 4, 2
B = 128
NB = 4
PAIRS = [(i, j) for i in range(NB) for j in range(i, NB)]
HALF = len(PAIRS) // 2

TN = (((0,), (0,)), ((), ()))


def dot(a, b, dims):
    return lax.dot_general(a, b, dims, preferred_element_type=jnp.float32)


def sketch_kernel(me_ref, d_ref, m_ref, s_ref, p_ref, hl_ref, g_ref, a_ref):
    k = p_ref.shape[1]
    c = ((d_ref[...].astype(jnp.float32) - m_ref[...]) * s_ref[...]).astype(jnp.bfloat16)
    sketch = jnp.dot(c, p_ref[...], preferred_element_type=jnp.float32)
    hi = sketch.astype(jnp.bfloat16)
    lo = (sketch - hi.astype(jnp.float32)).astype(jnp.bfloat16)
    hl_ref[:, :k] = hi
    hl_ref[:, k:] = lo
    i = pl.program_id(0)

    @pl.when(i == 0)
    def _():
        a_ref[...] = dot(hi, hl_ref[...], TN)

    @pl.when(i > 0)
    def _():
        a_ref[...] += dot(hi, hl_ref[...], TN)

    @pl.when(i == pl.num_programs(0) - 1)
    def _():
        for n, (p, q) in enumerate(PAIRS):
            r, t = slice(p * B, (p + 1) * B), slice(q * B, (q + 1) * B)
            u, v = slice(k + p * B, k + (p + 1) * B), slice(k + q * B, k + (q + 1) * B)
            side = (n // HALF + me_ref[0]) & 1
            g_ref[side, n % HALF * B : (n % HALF + 1) * B, :] = a_ref[r, t] + (a_ref[r, v] + a_ref[t, u].T)


def sketch_gram(me, dosage, mean, scale, probes, step=512):
    n, m = dosage.shape
    k = probes.shape[1]
    whole = lambda i: (0, 0)
    return pl.pallas_call(
        sketch_kernel,
        grid=(n // step,),
        in_specs=[
            pl.BlockSpec(memory_space=pltpu.SMEM),
            pl.BlockSpec((step, m), lambda i: (i, 0)),
            pl.BlockSpec((1, m), whole),
            pl.BlockSpec((1, m), whole),
            pl.BlockSpec((m, k), whole),
        ],
        out_specs=(
            pl.BlockSpec((step, 2 * k), lambda i: (i, 0)),
            pl.BlockSpec((NC, HALF * B, B), lambda i: (0, 0, 0)),
        ),
        out_shape=(
            jax.ShapeDtypeStruct((n, 2 * k), jnp.bfloat16),
            jax.ShapeDtypeStruct((NC, HALF * B, B), jnp.float32),
        ),
        scratch_shapes=[pltpu.VMEM((k, 2 * k), jnp.float32)],
        name="sketch_gram",
    )(me, dosage, mean, scale, probes)


def product_kernel(d_ref, m_ref, s_ref, hl_ref, *refs):
    w_ref = refs[-1]
    k = w_ref.shape[1]
    c = ((d_ref[...].astype(jnp.float32) - m_ref[...]) * s_ref[...]).astype(jnp.bfloat16)
    both = dot(c, hl_ref[...], TN)
    w_ref[...] = both[:, :k] + both[:, k:]


def product(part, dosage, mean, scale, hl, *earlier, step=512):
    n, m = dosage.shape
    k = hl.shape[1] // 2
    steps = m // step // 2
    off = part * steps
    return pl.pallas_call(
        product_kernel,
        grid=(steps,),
        in_specs=[
            pl.BlockSpec((n, step), lambda i: (0, i + off)),
            pl.BlockSpec((1, step), lambda i: (0, i + off)),
            pl.BlockSpec((1, step), lambda i: (0, i + off)),
            pl.BlockSpec((n, 2 * k), lambda i: (0, 0)),
        ]
        + [pl.BlockSpec(memory_space=pl.ANY)] * part,
        out_specs=pl.BlockSpec((step, k), lambda i: (i + off, 0)),
        out_shape=jax.ShapeDtypeStruct((m, k), jnp.float32),
        input_output_aliases={4: 0} if part else {},
        cost_estimate=pl.CostEstimate(
            flops=2 * n * m * k, bytes_accessed=12 << 20, transcendentals=0
        ),
    )(dosage, mean, scale, hl, *earlier)


def gather_kernel(flip, me_ref, i_ref, w_ref, *refs):
    o_ref = refs[-1]
    c = (me_ref[0] + flip) & 1

    def block(n, _):
        base = 32 * ((n & 7) * (NY * NC) + ((n >> 3) & 3) * NC + c) + 8 * (n >> 5)
        at = pl.ds(pl.multiple_of(n * 8, 8), 8)
        rows = jnp.concatenate([w_ref[pl.ds(i_ref[base + s], 1), :] for s in range(8)], axis=0)
        o_ref[at, :] = rows if flip else rows + refs[0][at, :]
        return 0

    lax.fori_loop(0, NX * NY * NZ, block, 0, unroll=4)


def gather_rows(flip, me, perm, rows, *came):
    sm, vm = pl.BlockSpec(memory_space=pltpu.SMEM), pl.BlockSpec(memory_space=pltpu.VMEM)
    return pl.pallas_call(
        functools.partial(gather_kernel, flip),
        out_shape=jax.ShapeDtypeStruct((rows.shape[0] // NC, rows.shape[1]), rows.dtype),
        in_specs=[sm, sm, vm] + [vm] * len(came),
        out_specs=vm,
        cost_estimate=pl.CostEstimate(flops=6_000_000_000, bytes_accessed=8 << 20, transcendentals=0),
    )(me, perm, rows, *came)


HI = lax.Precision.HIGHEST
NT = (((1,), (1,)), ((), ()))


def factor_kernel(p, me_ref, near_ref, far_ref, *refs):
    prior = refs[:p]
    r_ref, inv_ref, s_ref = refs[p:]
    w = (NB - p) * B
    wide = w + B
    for t in range(NB - p):
        n = PAIRS.index((p, p + t))
        at = slice(n % HALF * B, (n % HALF + 1) * B)
        near = (n // HALF + me_ref[0]) & 1 == 0
        s_ref[:, t * B : (t + 1) * B] = jnp.where(near, near_ref[at, :], far_ref[at, :])
    for q in range(p):
        off = (p - q) * B
        s_ref[:, :w] -= lax.dot_general(
            prior[q][:, off : off + B], prior[q][:, off:], TN,
            precision=HI, preferred_element_type=jnp.float32)
    s_ref[:, w:] = (
        lax.broadcasted_iota(jnp.int32, (B, B), 0) == lax.broadcasted_iota(jnp.int32, (B, B), 1)
    ).astype(jnp.float32)
    for b in range(B // 8):
        lo = 8 * b
        rows = s_ref[lo : lo + 8, :]
        cols = [jnp.broadcast_to(rows[:, lo + m : lo + m + 1], (8, B)) for m in range(8)]
        e = [[jnp.broadcast_to(cols[m][j : j + 1, :], (8, B)) if j >= m else None
              for m in range(8)] for j in range(8)]
        u = [[jnp.broadcast_to(rows[j : j + 1, t * B : (t + 1) * B], (8, B))
              for t in range(wide // B)] for j in range(8)]
        inv = [None] * 8
        l = [[None] * 8 for _ in range(8)]
        for j in range(8):
            inv[j] = 1.0 / e[j][j]
            for m in range(j + 1, 8):
                l[m][j] = e[m][j] * inv[j]
            for m in range(j + 1, 8):
                for n in range(m, 8):
                    e[n][m] = e[n][m] - l[n][j] * e[m][j]
                u[m] = [a - l[m][j] * c for a, c in zip(u[m], u[j])]
        v = [[a * inv[j] for a in u[j]] for j in range(8)]
        for j in range(8):
            root = lax.rsqrt(e[j][j])
            root = root * (1.5 - 0.5 * e[j][j] * root * root)
            for t in range(wide // B):
                row = (u[j][t] * root)[0:1, :]
                if t < NB - p:
                    r_ref[lo + j : lo + j + 1, t * B : (t + 1) * B] = row
                else:
                    inv_ref[lo + j : lo + j + 1, :] = row
        for d in range(b + 1, B // 8):
            at = slice(8 * d, 8 * d + 8)
            tail = s_ref[at, :]
            cols = [jnp.broadcast_to(tail[:, lo + m : lo + m + 1], (8, B)) for m in range(8)]
            for j in range(8):
                for m in range(j + 1, 8):
                    cols[m] = cols[m] - cols[j] * l[m][j]
            for t in range(wide // B):
                x = tail[:, t * B : (t + 1) * B]
                y = cols[0] * v[0][t]
                z = cols[1] * v[1][t]
                for m in range(2, 8, 2):
                    y = y + cols[m] * v[m][t]
                    z = z + cols[m + 1] * v[m + 1][t]
                s_ref[at, t * B : (t + 1) * B] = x - (y + z)


def factor(p, me, near, far, prior):
    w = (NB - p) * B
    vm = pl.BlockSpec(memory_space=pltpu.VMEM)
    return pl.pallas_call(
        functools.partial(factor_kernel, p),
        out_shape=(
            jax.ShapeDtypeStruct((B, w), jnp.float32),
            jax.ShapeDtypeStruct((B, B), jnp.float32),
        ),
        in_specs=[pl.BlockSpec(memory_space=pltpu.SMEM)] + [vm] * (2 + p),
        out_specs=(vm, vm),
        scratch_shapes=[pltpu.VMEM((B, w + B), jnp.float32)],
        cost_estimate=pl.CostEstimate(flops=10_000_000_000, bytes_accessed=1 << 20, transcendentals=0),
    )(me, near, far, *prior)


def finish_kernel(w_ref, *refs):
    r, inv, x_ref = refs[:NB], refs[NB : 2 * NB], refs[2 * NB]
    for p in range(NB):
        acc = w_ref[:, p * B : (p + 1) * B]
        for q in range(p):
            acc = acc - lax.dot_general(
                x_ref[:, q * B : (q + 1) * B], r[q][:, (p - q) * B : (p - q + 1) * B],
                (((1,), (0,)), ((), ())), precision=HI, preferred_element_type=jnp.float32)
        x_ref[:, p * B : (p + 1) * B] = lax.dot_general(
            acc, inv[p][...], NT, precision=HI, preferred_element_type=jnp.float32)


def finish(owned, panels, inverses):
    vm = pl.BlockSpec(memory_space=pltpu.VMEM)
    return pl.pallas_call(
        finish_kernel,
        out_shape=jax.ShapeDtypeStruct(owned.shape, jnp.float32),
        in_specs=[vm] * (1 + 2 * NB),
        out_specs=vm,
        name="finish",
    )(owned, *panels, *inverses)


def shifted(value, axis, size, step):
    return lax.ppermute(value, axis, [(k, (k + step) % size) for k in range(size)])


def swap(value, axes):
    return lax.all_to_all(value, axes, 0, 0, tiled=True)


def copies(value, count):
    return jnp.broadcast_to(value[None], (count,) + value.shape)


def after(value, *others):
    return lax.optimization_barrier((value,) + others)


def steps(dosage, allele_freq, probes, owner_perm):
    c = lax.axis_index("c")
    me = jnp.full((1,), c, jnp.int32)
    mean_dose = (2.0 * allele_freq)[None, :]
    inv_spread = (1.0 / jnp.sqrt(2.0 * allele_freq * (1.0 - allele_freq)))[None, :]
    both, packed = sketch_gram(me, dosage, mean_dose, inv_spread, probes)
    half = packed[0] + shifted(packed[1], "c", NC, 1)
    half, both = after(half, both)
    part = swap(half.reshape(NX * NY, -1, B), ("x", "y"))
    rows = product(0, dosage, mean_dose, inv_spread, both)
    part, rows = after(part.sum(0), rows)
    part = swap(copies(part, NZ), "z")
    rows = product(1, dosage, mean_dose, inv_spread, both, rows)
    part, rows = after(part.sum(0), rows)
    near = swap(copies(part, NX * NY), ("x", "y")).reshape(-1, B)
    away = gather_rows(1, me, owner_perm, rows)
    near, away = after(near, away)
    far = shifted(near, "c", NC, 1)
    came = shifted(away, "c", NC, 1)
    kept = gather_rows(0, me, owner_perm, rows, came)
    k = rows.shape[1]
    near, kept = after(near, kept)
    owned = swap(kept.reshape(NX * NY, -1, k), ("x", "y"))
    panels, inverses = [], []
    for p in range(NB):
        r, inv = factor(p, me, near, far, panels)
        panels.append(r)
        inverses.append(inv)
    owned = owned.sum(0).reshape(NZ, -1, k)
    owned = swap(copies(owned, NX).reshape(NX * NZ, -1, k), ("x", "z"))
    owned = owned.reshape(NX, NZ, -1, k).sum(1).reshape(-1, k)
    return finish(owned, panels, inverses)


def solution(mesh):
    torus = Mesh(mesh.devices.reshape(NX, NZ, NY, NC), ("x", "z", "y", "c"))
    return jax.shard_map(
        steps,
        mesh=torus,
        in_specs=(P(("x", "z", "y", "c"), None), P(), P(), P()),
        out_specs=P(("z", "y", "c"), None),
        check_vma=False,
    )
```

time: 172 us -> 146 us (0.85)
  local copies, waits for them, and re-layouts: 17.4 us -> 5.34 us
  waiting for transfers between devices: 35.4 us -> 23.7 us
  other arithmetic: 9.07 us -> 3.95 us
  Pallas kernels: 71.1 us -> 73.7 us
    gather x1 -> x0, local copies, waits for them, and re-layouts: 11.8 us -> none  [row_order(): return owner_perm.at[row.reshape(-1)].get(mode='promise_in_bounds')]
    ppermute x12 -> x3, waiting for transfers between devices: 17.1 us -> 5.48 us  [shifted(): lax.ppermute(value, axis, [(k, (k + step) % size) for k in range(size)])]
    ppermute x12 -> x3, starting transfers between devices: 12.2 us -> 0.6 us  [shifted(): lax.ppermute(value, axis, [(k, (k + step) % size) for k in range(size)])]
    all_to_all x3 -> x5, starting transfers between devices: 25.3 us -> 36.1 us  [swap(): return lax.all_to_all(value, axes, 0, 0, tiled=True)]
    add x7 -> x1, other arithmetic: 6.61 us -> 1.79 us  [steps(): half = packed[0] + shifted(packed[1], 'c', NC, 1)]
    pallas_call x4 -> x5, Pallas kernels: 40.2 us -> 42.8 us  [the longest x2 17.9 us: product(): pl.pallas_call(product_kernel, grid=(steps,), in_specs=[pl.BlockSpec((n,...]
    all_to_all x3 -> x5, waiting for transfers between devices: 18.2 us -> 18.2 us  [swap(): return lax.all_to_all(value, axes, 0, 0, tiled=True)]
  transfers between devices with their start and end apart: 15 -> 8, of which waited for: 6 -> 6; matrix products, arithmetic and copies ran while one was open for 2% -> 0% of each run, Pallas kernels for 27% -> 41%
where the time goes in v2:
time: 146 us; the launch traced here: 143 us
  Pallas kernels  73.7 us (50%)
  starting transfers between devices  36.7 us (25%)
  waiting for transfers between devices  23.7 us (16%)
  local copies, waits for them, and re-layouts  5.34 us (4%)
  other arithmetic  3.95 us (3%)
    all_to_all x5, starting transfers between devices, swap(): return lax.all_to_all(value, axes, 0, 0, tiled=True)  36.1 us
    pallas_call x4, Pallas kernels, factor(): pl.pallas_call(functools.partial(factor_kernel, p), out_shape=(jax.ShapeD...  27.4 us
    all_to_all x5, waiting for transfers between devices, swap(): return lax.all_to_all(value, axes, 0, 0, tiled=True)  18.2 us
    pallas_call x2, Pallas kernels, product(): pl.pallas_call(product_kernel, grid=(steps,), in_specs=[pl.BlockSpec((n,...  17.9 us
    pallas_call x2, Pallas kernels, gather_rows(): pl.pallas_call(functools.partial(gather_kernel, flip), out_shape=jax.Shap...  13 us
    pallas_call x1, Pallas kernels, sketch_gram(): pl.pallas_call(sketch_kernel, grid=(n // step,), in_specs=[pl.BlockSpec(m...  11.8 us
    ppermute x3, waiting for transfers between devices, shifted(): lax.ppermute(value, axis, [(k, (k + step) % size) for k in range(size)])  5.48 us
    pallas_call x1, Pallas kernels, finish(): pl.pallas_call(finish_kernel, out_shape=jax.ShapeDtypeStruct(owned.shape,...  3.49 us
  transfers between devices with their start and end apart: 8, of which 6 were waited for; matrix products, arithmetic and copies ran while one was open for 0% of the time, Pallas kernels for 41%

profile of v2, /device:TPU:8, one launch (start us, length us, event | category | flops | bytes accessed | tf_op | source)
XLA Modules:
  0.0 143.5 jit_solution(2165204853438049851)
XLA Ops:
  0.0 1.3 multiply_rsqrt_fusion
  1.3 11.8 %sketch_gram.1 = (bf16[2048,1024]{1,0:T(8,128)(2,1)}, f32[2,640,128]{2,1,0:T(8,128)}) custom-call(s32[1]{0:T(128)} %bitcast.me_ref, bf16[2048,2048]{1,0:T(8,128)(2,1)} %d_ref.5, f32[1,2048]{1,0:T(1,128)} %bitcast.26, f32[1,2048]{1,0:T(1,128)} %bitcast.23, bf16[2048,512]{1,0:T(8,128)(2,1)} %p_ref.1), custom_call_target="tpu_custom_call" | custom-call | tf_op jit(solution)/shard_map/sketch_gram/pallas_call | solution.py:55
  13.1 1.0 slice_bitcast_fusion
  14.2 1.6 %collective-permute-done = f32[640,128]{1,0:T(8,128)S(1)} collective-permute-done((f32[640,128]{1,0:T(8,128)S(1)}, f32[640,128]{1,0:T(8,128)S(1)}, u32[]{:S(2)}, u32[]{:S(2)}) %collective-permute-start) | collective-permute-done | bytes 327712 | tf_op jit(solution)/shard_map/ppermute | solution.py:242
  15.8 1.8 %bitcast_add_fusion = f32[640,128]{1,0:T(8,128)} fusion(f32[640,128]{1,0:T(8,128)S(1)} %collective-permute-done, f32[2,640,128]{2,1,0:T(8,128)} %get-tuple-element.25), kind=kLoop, calls=%fused_computation.1 | loop fusion | flops 81920 | bytes 983040 | tf_op jit(solution)/shard_map/add | solution.py:263
  17.6 7.4 %all-to-all-start = ((f32[16,40,128]{2,1,0:T(8,128)}), f32[16,40,128]{2,1,0:T(8,128)S(1)}, u32[]{:S(2)}, u32[]{:S(2)}) async-start(f32[16,40,128]{2,1,0:T(8,128)} %bitcast.5), calls=%async_computation | async-start | bytes 655360 | tf_op jit(solution)/shard_map/all_to_all | solution.py:246
  25.0 9.3 %shard_map.46.refs_0_ = f32[2048,512]{1,0:T(8,128)} custom-call(bf16[2048,2048]{1,0:T(8,128)(2,1)} %d_ref.5, f32[1,2048]{1,0:T(1,128)} %bitcast.27, f32[1,2048]{1,0:T(1,128)} %bitcast.24, bf16[2048,1024]{1,0:T(8,128)(2,1)} %get-tuple-element.28.hl_ref), custom_call_target="tpu_custom_call" | custom-call | flops 4294967296 | bytes 12582912 | tf_op jit(solution)/shard_map/pallas_call | solution.py:91
  34.3 0.7 broadcast_in_dim.31
  35.0 8.5 %all-to-all-start.1 = ((f32[8,40,128]{2,1,0:T(8,128)}), f32[8,40,128]{2,1,0:T(8,128)S(1)}, u32[]{:S(2)}, u32[]{:S(2)}) async-start(f32[8,40,128]{2,1,0:T(8,128)} %broadcast_in_dim.31), calls=%async_computation.1 | async-start | bytes 327680 | tf_op jit(solution)/shard_map/all_to_all | solution.py:246
  43.5 8.7 %shard_map.47.w_ref = f32[2048,512]{1,0:T(8,128)} custom-call(bf16[2048,2048]{1,0:T(8,128)(2,1)} %d_ref.5, f32[1,2048]{1,0:T(1,128)} %bitcast.28, f32[1,2048]{1,0:T(1,128)} %bitcast.25, bf16[2048,1024]{1,0:T(8,128)(2,1)} %get-tuple-element.28.hl_ref, f32[2048,512]{1,0:T(8,128)} %shard_map.46.refs_0_), custom_call_target="tpu_custom_call", output_to_operand_aliasing={{}: (4, {})} | custom-call | flops 4294967296 | bytes 12582912 | tf_op jit(solution)/shard_map/pallas_call | solution.py:91
  52.1 0.9 all-to-all-done.1
  53.0 0.8 broadcast_in_dim.32
  53.8 7.2 %all-to-all-start.2 = ((f32[16,40,128]{2,1,0:T(8,128)}), f32[16,40,128]{2,1,0:T(8,128)S(1)}, u32[]{:S(2)}, u32[]{:S(2)}) async-start(f32[16,40,128]{2,1,0:T(8,128)} %broadcast_in_dim.32), calls=%async_computation.2 | async-start | bytes 655360 | tf_op jit(solution)/shard_map/all_to_all | solution.py:246
  61.0 6.2 %shard_map.48 = f32[1024,512]{1,0:T(8,128)} custom-call(s32[1]{0:T(128)} %bitcast.me_ref, s32[2048]{0:T(1024)} %i_ref.3, f32[2048,512]{1,0:T(8,128)} %shard_map.47.w_ref), custom_call_target="tpu_custom_call" | custom-call | flops 6000000000 | bytes 8388608 | tf_op jit(solution)/shard_map/pallas_call | solution.py:126
  67.2 1.1 all-to-all-done.2
  68.3 0.5 collective-permute-start.2
  68.8 3.9 %collective-permute-done.1.refs_0_ = f32[1024,512]{1,0:T(8,128)S(1)} collective-permute-done((f32[1024,512]{1,0:T(8,128)}, f32[1024,512]{1,0:T(8,128)S(1)}, u32[]{:S(2)}, u32[]{:S(2)}) %collective-permute-start.1) | collective-permute-done | bytes 2097184 | tf_op jit(solution)/shard_map/ppermute | solution.py:242
  72.7 1.3 copy-done.1
  74.0 6.9 %shard_map.49 = f32[1024,512]{1,0:T(8,128)} custom-call(s32[1]{0:T(128)} %bitcast.me_ref, s32[2048]{0:T(1024)} %i_ref.3, f32[2048,512]{1,0:T(8,128)} %shard_map.47.w_ref, f32[1024,512]{1,0:T(8,128)} %copy-done.1), custom_call_target="tpu_custom_call" | custom-call | flops 6000000000 | bytes 8388608 | tf_op jit(solution)/shard_map/pallas_call | solution.py:126
  80.9 6.1 %all-to-all-start.3 = ((f32[16,64,512]{2,1,0:T(8,128)}), f32[16,64,512]{2,1,0:T(8,128)S(1)}, u32[]{:S(2)}, u32[]{:S(2)}) async-start(f32[16,64,512]{2,1,0:T(8,128)} %bitcast.15), calls=%async_computation.3 | async-start | bytes 4194304 | tf_op jit(solution)/shard_map/all_to_all | solution.py:246
  87.0 0.7 copy-done.2
  87.7 6.9 %shard_map.50 = (f32[128,512]{1,0:T(8,128)}, f32[128,128]{1,0:T(8,128)}) custom-call(s32[1]{0:T(128)} %bitcast.me_ref, f32[640,128]{1,0:T(8,128)} %bitcast.18, f32[640,128]{1,0:T(8,128)} %copy-done.2), custom_call_target="tpu_custom_call" | custom-call | flops 10000000000 | bytes 1048576 | tf_op jit(solution)/shard_map/pallas_call | solution.py:205
  94.6 7.1 %shard_map.51 = (f32[128,384]{1,0:T(8,128)}, f32[128,128]{1,0:T(8,128)}) custom-call(s32[1]{0:T(128)} %bitcast.me_ref, f32[640,128]{1,0:T(8,128)} %bitcast.19, f32[640,128]{1,0:T(8,128)} %copy-done.2, f32[128,512]{1,0:T(8,128)} %get-tuple-element.37.refs_0_), custom_call_target="tpu_custom_call" | custom-call | flops 10000000000 | bytes 1048576 | tf_op jit(solution)/shard_map/pallas_call | solution.py:205
  101.6 15.1 %all-to-all-done.3 = f32[16,64,512]{2,1,0:T(8,128)S(1)} async-done(((f32[16,64,512]{2,1,0:T(8,128)}), f32[16,64,512]{2,1,0:T(8,128)S(1)}, u32[]{:S(2)}, u32[]{:S(2)}) %all-to-all-start.3) | async-done | bytes 2097184 | tf_op jit(solution)/shard_map/all_to_all | solution.py:246
  116.7 0.2 reduce_sum.38
  116.9 0.9 broadcast_in_dim.34
  117.8 7.0 %all-to-all-start.4 = ((f32[32,8,512]{2,1,0:T(8,128)}), f32[32,8,512]{2,1,0:T(8,128)S(1)}, u32[]{:S(2)}, u32[]{:S(2)}) async-start(f32[32,8,512]{2,1,0:T(8,128)} %bitcast.9), calls=%async_computation.4 | async-start | bytes 1048576 | tf_op jit(solution)/shard_map/all_to_all | solution.py:246
  124.7 6.9 %shard_map.52 = (f32[128,256]{1,0:T(8,128)}, f32[128,128]{1,0:T(8,128)}) custom-call(s32[1]{0:T(128)} %bitcast.me_ref, f32[640,128]{1,0:T(8,128)} %bitcast.20, f32[640,128]{1,0:T(8,128)} %copy-done.2, f32[128,512]{1,0:T(8,128)} %get-tuple-element.37.refs_0_, f32[128,384]{1,0:T(8,128)} %get-tuple-element.38.refs_1_), custom_call_target="tpu_custom_call" | custom-call | flops 10000000000 | bytes 1048576 | tf_op jit(solution)/shard_map/pallas_call | solution.py:205
  131.6 6.7 %shard_map.53 = (f32[128,128]{1,0:T(8,128)}, f32[128,128]{1,0:T(8,128)}) custom-call(s32[1]{0:T(128)} %bitcast.me_ref, f32[640,128]{1,0:T(8,128)} %bitcast.21, f32[640,128]{1,0:T(8,128)} %copy-done.2, f32[128,512]{1,0:T(8,128)} %get-tuple-element.37.refs_0_, f32[128,384]{1,0:T(8,128)} %get-tuple-element.38.refs_1_, f32[128,256]{1,0:T(8,128)} %get-tuple-element.39.refs_2_), custom_call_target="tpu_custom_call" | custom-call | flops 10000000000 | bytes 1048576 | tf_op jit(solution)/shard_map/pallas_call | solution.py:205
  138.3 1.1 all-to-all-done.4
  139.3 0.7 bitcast_reduce_fusion
  140.0 3.5 %finish.1 = f32[32,512]{1,0:T(8,128)} custom-call(f32[32,512]{1,0:T(8,128)} %bitcast.22, f32[128,512]{1,0:T(8,128)} %get-tuple-element.37.refs_0_, f32[128,384]{1,0:T(8,128)} %get-tuple-element.38.refs_1_, f32[128,256]{1,0:T(8,128)} %get-tuple-element.39.refs_2_, f32[128,128]{1,0:T(8,128)} %get-tuple-element.40.refs_3_, ...), custom_call_target="tpu_custom_call" | custom-call | tf_op jit(solution)/shard_map/finish/pallas_call | solution.py:232
  (10 shorter events, 0.1 us)
Async XLA Ops:
  14.1 1.7 %collective-permute-start = (f32[640,128]{1,0:T(8,128)S(1)}, f32[640,128]{1,0:T(8,128)S(1)}, u32[]{:S(2)}, u32[]{:S(2)}) collective-permute-start(f32[640,128]{1,0:T(8,128)S(1)} %slice_bitcast_fusion), channel_id=1, source_target_pairs={{0,1},{1,0},{2,3},{3,2},{4,5},{5,4},{6,7},{7,6},{8,9},{9,8},{10,11... | collective-permute-start | bytes 983048 | tf_op jit(solution)/shard_map/ppermute | solution.py:242
  17.6 16.7 %all-to-all-start = ((f32[16,40,128]{2,1,0:T(8,128)}), f32[16,40,128]{2,1,0:T(8,128)S(1)}, u32[]{:S(2)}, u32[]{:S(2)}) async-start(f32[16,40,128]{2,1,0:T(8,128)} %bitcast.5), calls=%async_computation | async-start | bytes 655360 | tf_op jit(solution)/shard_map/all_to_all | solution.py:246
  35.0 18.0 %all-to-all-start.1 = ((f32[8,40,128]{2,1,0:T(8,128)}), f32[8,40,128]{2,1,0:T(8,128)S(1)}, u32[]{:S(2)}, u32[]{:S(2)}) async-start(f32[8,40,128]{2,1,0:T(8,128)} %broadcast_in_dim.31), calls=%async_computation.1 | async-start | bytes 327680 | tf_op jit(solution)/shard_map/all_to_all | solution.py:246
  53.8 14.5 %all-to-all-start.2 = ((f32[16,40,128]{2,1,0:T(8,128)}), f32[16,40,128]{2,1,0:T(8,128)S(1)}, u32[]{:S(2)}, u32[]{:S(2)}) async-start(f32[16,40,128]{2,1,0:T(8,128)} %broadcast_in_dim.32), calls=%async_computation.2 | async-start | bytes 655360 | tf_op jit(solution)/shard_map/all_to_all | solution.py:246
  68.3 12.6 %copy-start = (f32[16,40,128]{2,1,0:T(8,128)}, f32[16,40,128]{2,1,0:T(8,128)S(1)}, u32[]{:S(2)}) copy-start(f32[16,40,128]{2,1,0:T(8,128)S(1)} %all-to-all-done.2) | copy-start | bytes 983044
  68.3 4.4 %collective-permute-start.1 = (f32[1024,512]{1,0:T(8,128)}, f32[1024,512]{1,0:T(8,128)S(1)}, u32[]{:S(2)}, u32[]{:S(2)}) collective-permute-start(f32[1024,512]{1,0:T(8,128)} %shard_map.48), channel_id=1, source_target_pairs={{0,1},{1,0},{2,3},{3,2},{4,5},{5,4},{6,7},{7,6},{8,9},{9,8},{10,11... | collective-permute-start | bytes 6291464 | tf_op jit(solution)/shard_map/ppermute | solution.py:242
  68.3 18.7 %collective-permute-start.2 = (f32[640,128]{1,0:T(8,128)S(1)}, f32[640,128]{1,0:T(8,128)S(1)}, u32[]{:S(2)}, u32[]{:S(2)}) collective-permute-start(f32[640,128]{1,0:T(8,128)S(1)} %bitcast.17), channel_id=1, source_target_pairs={{0,1},{1,0},{2,3},{3,2},{4,5},{5,4},{6,7},{7,6},{8,9},{9,8},{10,11... | collective-permute-start | bytes 983048 | tf_op jit(solution)/shard_map/ppermute | solution.py:242
  72.7 1.3 copy-start.1
  80.9 35.9 %all-to-all-start.3 = ((f32[16,64,512]{2,1,0:T(8,128)}), f32[16,64,512]{2,1,0:T(8,128)S(1)}, u32[]{:S(2)}, u32[]{:S(2)}) async-start(f32[16,64,512]{2,1,0:T(8,128)} %bitcast.15), calls=%async_computation.3 | async-start | bytes 4194304 | tf_op jit(solution)/shard_map/all_to_all | solution.py:246
  87.0 0.7 copy-start.2
  117.8 21.6 %all-to-all-start.4 = ((f32[32,8,512]{2,1,0:T(8,128)}), f32[32,8,512]{2,1,0:T(8,128)S(1)}, u32[]{:S(2)}, u32[]{:S(2)}) async-start(f32[32,8,512]{2,1,0:T(8,128)} %bitcast.9), calls=%async_computation.4 | async-start | bytes 1048576 | tf_op jit(solution)/shard_map/all_to_all | solution.py:246

commit v3 on v2

--- a/solution.py
+++ b/solution.py
@@ -21,7 +21,7 @@
     return lax.dot_general(a, b, dims, preferred_element_type=jnp.float32)
 
 
-def sketch_kernel(me_ref, d_ref, m_ref, s_ref, p_ref, hl_ref, g_ref, a_ref):
+def sketch_kernel(me_ref, d_ref, m_ref, s_ref, p_ref, hl_ref, near_ref, far_ref, a_ref):
     k = p_ref.shape[1]
     c = ((d_ref[...].astype(jnp.float32) - m_ref[...]) * s_ref[...]).astype(jnp.bfloat16)
     sketch = jnp.dot(c, p_ref[...], preferred_element_type=jnp.float32)
@@ -41,11 +41,17 @@
 
     @pl.when(i == pl.num_programs(0) - 1)
     def _():
-        for n, (p, q) in enumerate(PAIRS):
+        def block(p, q):
             r, t = slice(p * B, (p + 1) * B), slice(q * B, (q + 1) * B)
             u, v = slice(k + p * B, k + (p + 1) * B), slice(k + q * B, k + (q + 1) * B)
-            side = (n // HALF + me_ref[0]) & 1
-            g_ref[side, n % HALF * B : (n % HALF + 1) * B, :] = a_ref[r, t] + (a_ref[r, v] + a_ref[t, u].T)
+            return a_ref[r, t] + (a_ref[r, v] + a_ref[t, u].T)
+
+        first = me_ref[0] == 0
+        for n in range(HALF):
+            at = slice(n * B, (n + 1) * B)
+            a, b = block(*PAIRS[n]), block(*PAIRS[n + HALF])
+            near_ref[at, :] = jnp.where(first, a, b)
+            far_ref[at, :] = jnp.where(first, b, a)
 
 
 def sketch_gram(me, dosage, mean, scale, probes, step=512):
@@ -64,47 +70,45 @@
         ],
         out_specs=(
             pl.BlockSpec((step, 2 * k), lambda i: (i, 0)),
-            pl.BlockSpec((NC, HALF * B, B), lambda i: (0, 0, 0)),
+            pl.BlockSpec((HALF * B, B), whole),
+            pl.BlockSpec((HALF * B, B), whole),
         ),
         out_shape=(
             jax.ShapeDtypeStruct((n, 2 * k), jnp.bfloat16),
-            jax.ShapeDtypeStruct((NC, HALF * B, B), jnp.float32),
+            jax.ShapeDtypeStruct((HALF * B, B), jnp.float32),
+            jax.ShapeDtypeStruct((HALF * B, B), jnp.float32),
         ),
         scratch_shapes=[pltpu.VMEM((k, 2 * k), jnp.float32)],
         name="sketch_gram",
     )(me, dosage, mean, scale, probes)
 
 
-def product_kernel(d_ref, m_ref, s_ref, hl_ref, *refs):
-    w_ref = refs[-1]
+def product_kernel(d_ref, m_ref, s_ref, hl_ref, w_ref):
     k = w_ref.shape[1]
     c = ((d_ref[...].astype(jnp.float32) - m_ref[...]) * s_ref[...]).astype(jnp.bfloat16)
     both = dot(c, hl_ref[...], TN)
     w_ref[...] = both[:, :k] + both[:, k:]
 
 
-def product(part, dosage, mean, scale, hl, *earlier, step=512):
+def product(dosage, mean, scale, hl, step=512):
     n, m = dosage.shape
     k = hl.shape[1] // 2
-    steps = m // step // 2
-    off = part * steps
     return pl.pallas_call(
         product_kernel,
-        grid=(steps,),
+        grid=(m // step,),
         in_specs=[
-            pl.BlockSpec((n, step), lambda i: (0, i + off)),
-            pl.BlockSpec((1, step), lambda i: (0, i + off)),
-            pl.BlockSpec((1, step), lambda i: (0, i + off)),
+            pl.BlockSpec((n, step), lambda i: (0, i)),
+            pl.BlockSpec((1, step), lambda i: (0, i)),
+            pl.BlockSpec((1, step), lambda i: (0, i)),
             pl.BlockSpec((n, 2 * k), lambda i: (0, 0)),
-        ]
-        + [pl.BlockSpec(memory_space=pl.ANY)] * part,
-        out_specs=pl.BlockSpec((step, k), lambda i: (i + off, 0)),
+        ],
+        out_specs=pl.BlockSpec((step, k), lambda i: (i, 0)),
         out_shape=jax.ShapeDtypeStruct((m, k), jnp.float32),
-        input_output_aliases={4: 0} if part else {},
+        name="product",
         cost_estimate=pl.CostEstimate(
-            flops=2 * n * m * k, bytes_accessed=12 << 20, transcendentals=0
+            flops=4 * n * m * k, bytes_accessed=16 << 20, transcendentals=0
         ),
-    )(dosage, mean, scale, hl, *earlier)
+    )(dosage, mean, scale, hl)
 
 
 def gather_kernel(flip, me_ref, i_ref, w_ref, *refs):
@@ -259,23 +263,21 @@
     me = jnp.full((1,), c, jnp.int32)
     mean_dose = (2.0 * allele_freq)[None, :]
     inv_spread = (1.0 / jnp.sqrt(2.0 * allele_freq * (1.0 - allele_freq)))[None, :]
-    both, packed = sketch_gram(me, dosage, mean_dose, inv_spread, probes)
-    half = packed[0] + shifted(packed[1], "c", NC, 1)
+    both, near, far = sketch_gram(me, dosage, mean_dose, inv_spread, probes)
+    half = near + shifted(far, "c", NC, 1)
     half, both = after(half, both)
     part = swap(half.reshape(NX * NY, -1, B), ("x", "y"))
-    rows = product(0, dosage, mean_dose, inv_spread, both)
+    rows = product(dosage, mean_dose, inv_spread, both)
     part, rows = after(part.sum(0), rows)
     part = swap(copies(part, NZ), "z")
-    rows = product(1, dosage, mean_dose, inv_spread, both, rows)
-    part, rows = after(part.sum(0), rows)
+    away = gather_rows(1, me, owner_perm, rows)
+    part, away = after(part.sum(0), away)
+    came = shifted(away, "c", NC, 1)
     near = swap(copies(part, NX * NY), ("x", "y")).reshape(-1, B)
-    away = gather_rows(1, me, owner_perm, rows)
-    near, away = after(near, away)
+    kept = gather_rows(0, me, owner_perm, rows, came)
+    near, kept = after(near, kept)
     far = shifted(near, "c", NC, 1)
-    came = shifted(away, "c", NC, 1)
-    kept = gather_rows(0, me, owner_perm, rows, came)
     k = rows.shape[1]
-    near, kept = after(near, kept)
     owned = swap(kept.reshape(NX * NY, -1, k), ("x", "y"))
     panels, inverses = [], []
     for p in range(NB):

time: 146 us -> 135 us (0.925)
  Pallas kernels: 73.7 us -> 69.2 us
  starting transfers between devices: 36.7 us -> 33.8 us
  waiting for transfers between devices: 23.7 us -> 21.7 us
  local copies, waits for them, and re-layouts: 5.34 us -> 3.79 us
    pallas_call x2 -> x1, Pallas kernels: 17.9 us -> 13.4 us  [product(): pl.pallas_call(product_kernel, grid=(m // step,), in_specs=[pl.BlockSpec(...]
    ppermute x3, waiting for transfers between devices: 5.48 us -> 1.84 us  [shifted(): lax.ppermute(value, axis, [(k, (k + step) % size) for k in range(size)])]
    all_to_all x5, starting transfers between devices: 36.1 us -> 33.7 us  [swap(): return lax.all_to_all(value, axes, 0, 0, tiled=True)]
    all_to_all x5, waiting for transfers between devices: 18.2 us -> 19.8 us  [swap(): return lax.all_to_all(value, axes, 0, 0, tiled=True)]
  transfers between devices with their start and end apart: 8 -> 8, of which waited for: 6 -> 5; matrix products, arithmetic and copies ran while one was open for 0% -> 1% of each run, Pallas kernels for 41% -> 41%
where the time goes in v3:
time: 135 us; the launch traced here: 132 us
  Pallas kernels  69.2 us (51%)
  starting transfers between devices  33.8 us (25%)
  waiting for transfers between devices  21.7 us (16%)
  other arithmetic  3.95 us (3%)
  local copies, waits for them, and re-layouts  3.79 us (3%)
    all_to_all x5, starting transfers between devices, swap(): return lax.all_to_all(value, axes, 0, 0, tiled=True)  33.7 us
    pallas_call x4, Pallas kernels, factor(): pl.pallas_call(functools.partial(factor_kernel, p), out_shape=(jax.ShapeD...  27.4 us
    all_to_all x5, waiting for transfers between devices, swap(): return lax.all_to_all(value, axes, 0, 0, tiled=True)  19.8 us
    pallas_call x1, Pallas kernels, product(): pl.pallas_call(product_kernel, grid=(m // step,), in_specs=[pl.BlockSpec(...  13.4 us
    pallas_call x2, Pallas kernels, gather_rows(): pl.pallas_call(functools.partial(gather_kernel, flip), out_shape=jax.Shap...  13 us
    pallas_call x1, Pallas kernels, sketch_gram(): pl.pallas_call(sketch_kernel, grid=(n // step,), in_specs=[pl.BlockSpec(m...  11.8 us
    pallas_call x1, Pallas kernels, finish(): pl.pallas_call(finish_kernel, out_shape=jax.ShapeDtypeStruct(owned.shape,...  3.49 us
  transfers between devices with their start and end apart: 8, of which 5 were waited for; matrix products, arithmetic and copies ran while one was open for 1% of the time, Pallas kernels for 41%

profile of v3, /device:TPU:8, one launch (start us, length us, event | category | flops | bytes accessed | tf_op | source)
XLA Modules:
  0.0 132.4 jit_solution(8177467128911253407)
XLA Ops:
  0.0 1.3 multiply_rsqrt_fusion
  1.3 11.8 %sketch_gram.1 = (bf16[2048,1024]{1,0:T(8,128)(2,1)}, f32[640,128]{1,0:T(8,128)}, f32[640,128]{1,0:T(8,128)}) custom-call(s32[1]{0:T(128)} %bitcast.me_ref, bf16[2048,2048]{1,0:T(8,128)(2,1)} %d_ref.3, f32[1,2048]{1,0:T(1,128)} %bitcast.21, f32[1,2048]{1,0:T(1,128)} %bitcast.19, bf16[2048,512]{1,0:T(8,128)(2,1)} %p_ref.1), custom_call_target="tpu_custom_call" | custom-call | tf_op jit(solution)/shard_map/sketch_gram/pallas_call | solution.py:61
  13.2 1.8 %collective-permute-done = f32[640,128]{1,0:T(8,128)S(1)} collective-permute-done((f32[640,128]{1,0:T(8,128)}, f32[640,128]{1,0:T(8,128)S(1)}, u32[]{:S(2)}, u32[]{:S(2)}) %collective-permute-start) | collective-permute-done | bytes 327712 | tf_op jit(solution)/shard_map/ppermute | solution.py:246
  15.0 1.8 %add.3 = f32[640,128]{1,0:T(8,128)} add(f32[640,128]{1,0:T(8,128)} %get-tuple-element.24, f32[640,128]{1,0:T(8,128)S(1)} %collective-permute-done) | non-fusion elementwise | flops 81920 | bytes 983040 | tf_op jit(solution)/shard_map/add | solution.py:267
  16.8 7.4 %all-to-all-start = ((f32[16,40,128]{2,1,0:T(8,128)}), f32[16,40,128]{2,1,0:T(8,128)S(1)}, u32[]{:S(2)}, u32[]{:S(2)}) async-start(f32[16,40,128]{2,1,0:T(8,128)} %bitcast.3), calls=%async_computation | async-start | bytes 655360 | tf_op jit(solution)/shard_map/all_to_all | solution.py:250
  24.2 13.4 %product.1.w_ref = f32[2048,512]{1,0:T(8,128)} custom-call(bf16[2048,2048]{1,0:T(8,128)(2,1)} %d_ref.3, f32[1,2048]{1,0:T(1,128)} %bitcast.22, f32[1,2048]{1,0:T(1,128)} %bitcast.20, bf16[2048,1024]{1,0:T(8,128)(2,1)} %get-tuple-element.28.hl_ref), custom_call_target="tpu_custom_call" | custom-call | flops 8589934592 | bytes 16777216 | tf_op jit(solution)/shard_map/product/pallas_call | solution.py:96
  37.6 0.7 broadcast_in_dim.31
  38.3 8.5 %all-to-all-start.1 = ((f32[8,40,128]{2,1,0:T(8,128)}), f32[8,40,128]{2,1,0:T(8,128)S(1)}, u32[]{:S(2)}, u32[]{:S(2)}) async-start(f32[8,40,128]{2,1,0:T(8,128)} %broadcast_in_dim.31), calls=%async_computation.1 | async-start | bytes 327680 | tf_op jit(solution)/shard_map/all_to_all | solution.py:250
  46.7 6.1 %shard_map.46 = f32[1024,512]{1,0:T(8,128)} custom-call(s32[1]{0:T(128)} %bitcast.me_ref, s32[2048]{0:T(1024)} %i_ref.3, f32[2048,512]{1,0:T(8,128)} %product.1.w_ref), custom_call_target="tpu_custom_call" | custom-call | flops 6000000000 | bytes 8388608 | tf_op jit(solution)/shard_map/pallas_call | solution.py:130
  52.9 3.4 %all-to-all-done.1 = f32[8,40,128]{2,1,0:T(8,128)S(1)} async-done(((f32[8,40,128]{2,1,0:T(8,128)}), f32[8,40,128]{2,1,0:T(8,128)S(1)}, u32[]{:S(2)}, u32[]{:S(2)}) %all-to-all-start.1) | async-done | bytes 163872 | tf_op jit(solution)/shard_map/all_to_all | solution.py:250
  56.3 0.1 collective-permute-start.1
  56.4 0.8 broadcast_in_dim.32
  57.2 7.2 %all-to-all-start.2 = ((f32[16,40,128]{2,1,0:T(8,128)}), f32[16,40,128]{2,1,0:T(8,128)S(1)}, u32[]{:S(2)}, u32[]{:S(2)}) async-start(f32[16,40,128]{2,1,0:T(8,128)} %broadcast_in_dim.32), calls=%async_computation.2 | async-start | bytes 655360 | tf_op jit(solution)/shard_map/all_to_all | solution.py:250
  64.4 0.0 collective-permute-done.1.refs_0_
  64.4 6.9 %shard_map.47 = f32[1024,512]{1,0:T(8,128)} custom-call(s32[1]{0:T(128)} %bitcast.me_ref, s32[2048]{0:T(1024)} %i_ref.3, f32[2048,512]{1,0:T(8,128)} %product.1.w_ref, f32[1024,512]{1,0:T(8,128)} %collective-permute-done.1.refs_0_), custom_call_target="tpu_custom_call" | custom-call | flops 6000000000 | bytes 8388608 | tf_op jit(solution)/shard_map/pallas_call | solution.py:130
  71.3 1.4 %all-to-all-done.2 = f32[16,40,128]{2,1,0:T(8,128)S(1)} async-done(((f32[16,40,128]{2,1,0:T(8,128)}), f32[16,40,128]{2,1,0:T(8,128)S(1)}, u32[]{:S(2)}, u32[]{:S(2)}) %all-to-all-start.2) | async-done | bytes 327712 | tf_op jit(solution)/shard_map/all_to_all | solution.py:250
  72.6 0.0 collective-permute-start.2
  72.6 0.7 copy-done
  73.4 5.9 %all-to-all-start.3 = ((f32[16,64,512]{2,1,0:T(8,128)}), f32[16,64,512]{2,1,0:T(8,128)S(1)}, u32[]{:S(2)}, u32[]{:S(2)}) async-start(f32[16,64,512]{2,1,0:T(8,128)} %bitcast.11), calls=%async_computation.3 | async-start | bytes 4194304 | tf_op jit(solution)/shard_map/all_to_all | solution.py:250
  79.2 0.0 collective-permute-done.2.far_ref
  79.2 0.7 copy-done.1
  80.0 6.9 %shard_map.48 = (f32[128,512]{1,0:T(8,128)}, f32[128,128]{1,0:T(8,128)}) custom-call(s32[1]{0:T(128)} %bitcast.me_ref, f32[640,128]{1,0:T(8,128)} %bitcast.14, f32[640,128]{1,0:T(8,128)} %copy-done.1), custom_call_target="tpu_custom_call" | custom-call | flops 10000000000 | bytes 1048576 | tf_op jit(solution)/shard_map/pallas_call | solution.py:209
  86.8 7.1 %shard_map.49 = (f32[128,384]{1,0:T(8,128)}, f32[128,128]{1,0:T(8,128)}) custom-call(s32[1]{0:T(128)} %bitcast.me_ref, f32[640,128]{1,0:T(8,128)} %bitcast.15, f32[640,128]{1,0:T(8,128)} %copy-done.1, f32[128,512]{1,0:T(8,128)} %get-tuple-element.35.refs_0_), custom_call_target="tpu_custom_call" | custom-call | flops 10000000000 | bytes 1048576 | tf_op jit(solution)/shard_map/pallas_call | solution.py:209
  93.9 14.6 %all-to-all-done.3 = f32[16,64,512]{2,1,0:T(8,128)S(1)} async-done(((f32[16,64,512]{2,1,0:T(8,128)}), f32[16,64,512]{2,1,0:T(8,128)S(1)}, u32[]{:S(2)}, u32[]{:S(2)}) %all-to-all-start.3) | async-done | bytes 2097184 | tf_op jit(solution)/shard_map/all_to_all | solution.py:250
  108.4 0.2 reduce_sum.38
  108.6 0.9 broadcast_in_dim.34
  109.5 4.7 %all-to-all-start.4 = ((f32[32,8,512]{2,1,0:T(8,128)}), f32[32,8,512]{2,1,0:T(8,128)S(1)}, u32[]{:S(2)}, u32[]{:S(2)}) async-start(f32[32,8,512]{2,1,0:T(8,128)} %bitcast.7), calls=%async_computation.4 | async-start | bytes 1048576 | tf_op jit(solution)/shard_map/all_to_all | solution.py:250
  114.2 6.8 %shard_map.50 = (f32[128,256]{1,0:T(8,128)}, f32[128,128]{1,0:T(8,128)}) custom-call(s32[1]{0:T(128)} %bitcast.me_ref, f32[640,128]{1,0:T(8,128)} %bitcast.16, f32[640,128]{1,0:T(8,128)} %copy-done.1, f32[128,512]{1,0:T(8,128)} %get-tuple-element.35.refs_0_, f32[128,384]{1,0:T(8,128)} %get-tuple-element.36.refs_1_), custom_call_target="tpu_custom_call" | custom-call | flops 10000000000 | bytes 1048576 | tf_op jit(solution)/shard_map/pallas_call | solution.py:209
  121.0 6.7 %shard_map.51 = (f32[128,128]{1,0:T(8,128)}, f32[128,128]{1,0:T(8,128)}) custom-call(s32[1]{0:T(128)} %bitcast.me_ref, f32[640,128]{1,0:T(8,128)} %bitcast.17, f32[640,128]{1,0:T(8,128)} %copy-done.1, f32[128,512]{1,0:T(8,128)} %get-tuple-element.35.refs_0_, f32[128,384]{1,0:T(8,128)} %get-tuple-element.36.refs_1_, f32[128,256]{1,0:T(8,128)} %get-tuple-element.37.refs_2_), custom_call_target="tpu_custom_call" | custom-call | flops 10000000000 | bytes 1048576 | tf_op jit(solution)/shard_map/pallas_call | solution.py:209
  127.7 0.5 all-to-all-done.4
  128.2 0.7 bitcast_reduce_fusion
  128.9 3.5 %finish.1 = f32[32,512]{1,0:T(8,128)} custom-call(f32[32,512]{1,0:T(8,128)} %bitcast.18, f32[128,512]{1,0:T(8,128)} %get-tuple-element.35.refs_0_, f32[128,384]{1,0:T(8,128)} %get-tuple-element.36.refs_1_, f32[128,256]{1,0:T(8,128)} %get-tuple-element.37.refs_2_, f32[128,128]{1,0:T(8,128)} %get-tuple-element.38.refs_3_, ...), custom_call_target="tpu_custom_call" | custom-call | tf_op jit(solution)/shard_map/finish/pallas_call | solution.py:236
  (6 shorter events, 0.0 us)
Async XLA Ops:
  13.2 1.8 %collective-permute-start = (f32[640,128]{1,0:T(8,128)}, f32[640,128]{1,0:T(8,128)S(1)}, u32[]{:S(2)}, u32[]{:S(2)}) collective-permute-start(f32[640,128]{1,0:T(8,128)} %get-tuple-element.25), channel_id=1, source_target_pairs={{0,1},{1,0},{2,3},{3,2},{4,5},{5,4},{6,7},{7,6},{8,9},{9,8},{10,11... | collective-permute-start | bytes 983048 | tf_op jit(solution)/shard_map/ppermute | solution.py:246
  16.8 20.8 %all-to-all-start = ((f32[16,40,128]{2,1,0:T(8,128)}), f32[16,40,128]{2,1,0:T(8,128)S(1)}, u32[]{:S(2)}, u32[]{:S(2)}) async-start(f32[16,40,128]{2,1,0:T(8,128)} %bitcast.3), calls=%async_computation | async-start | bytes 655360 | tf_op jit(solution)/shard_map/all_to_all | solution.py:250
  38.3 18.0 %all-to-all-start.1 = ((f32[8,40,128]{2,1,0:T(8,128)}), f32[8,40,128]{2,1,0:T(8,128)S(1)}, u32[]{:S(2)}, u32[]{:S(2)}) async-start(f32[8,40,128]{2,1,0:T(8,128)} %broadcast_in_dim.31), calls=%async_computation.1 | async-start | bytes 327680 | tf_op jit(solution)/shard_map/all_to_all | solution.py:250
  56.3 8.1 %collective-permute-start.1 = (f32[1024,512]{1,0:T(8,128)}, f32[1024,512]{1,0:T(8,128)}, u32[]{:S(2)}, u32[]{:S(2)}) collective-permute-start(f32[1024,512]{1,0:T(8,128)} %shard_map.46), channel_id=1, source_target_pairs={{0,1},{1,0},{2,3},{3,2},{4,5},{5,4},{6,7},{7,6},{8,9},{9,8},{10,11... | collective-permute-start | bytes 6291464 | tf_op jit(solution)/shard_map/ppermute | solution.py:246
  57.2 15.5 %all-to-all-start.2 = ((f32[16,40,128]{2,1,0:T(8,128)}), f32[16,40,128]{2,1,0:T(8,128)S(1)}, u32[]{:S(2)}, u32[]{:S(2)}) async-start(f32[16,40,128]{2,1,0:T(8,128)} %broadcast_in_dim.32), calls=%async_computation.2 | async-start | bytes 655360 | tf_op jit(solution)/shard_map/all_to_all | solution.py:250
  72.6 0.7 copy-start
  72.6 6.6 %collective-permute-start.2 = (f32[640,128]{1,0:T(8,128)S(1)}, f32[640,128]{1,0:T(8,128)S(1)}, u32[]{:S(2)}, u32[]{:S(2)}) collective-permute-start(f32[640,128]{1,0:T(8,128)S(1)} %bitcast.13), channel_id=1, source_target_pairs={{0,1},{1,0},{2,3},{3,2},{4,5},{5,4},{6,7},{7,6},{8,9},{9,8},{10,11... | collective-permute-start | bytes 983048 | tf_op jit(solution)/shard_map/ppermute | solution.py:246
  73.4 35.1 %all-to-all-start.3 = ((f32[16,64,512]{2,1,0:T(8,128)}), f32[16,64,512]{2,1,0:T(8,128)S(1)}, u32[]{:S(2)}, u32[]{:S(2)}) async-start(f32[16,64,512]{2,1,0:T(8,128)} %bitcast.11), calls=%async_computation.3 | async-start | bytes 4194304 | tf_op jit(solution)/shard_map/all_to_all | solution.py:250
  79.2 0.7 copy-start.1
  109.5 18.8 %all-to-all-start.4 = ((f32[32,8,512]{2,1,0:T(8,128)}), f32[32,8,512]{2,1,0:T(8,128)S(1)}, u32[]{:S(2)}, u32[]{:S(2)}) async-start(f32[32,8,512]{2,1,0:T(8,128)} %bitcast.7), calls=%async_computation.4 | async-start | bytes 1048576 | tf_op jit(solution)/shard_map/all_to_all | solution.py:250
